TPU v7x, 32 devices: a whole 2x2x4 slice. The times are simulated.
32 devices in a mesh: tbl: 16 (over z, x, core), hst: 2 (over y).
Axes of the slice: x: 2, y: 2, z: 4, core: 2. Of those that a mesh axis runs over, the one named last changes fastest.
Arguments:
- pooled: bfloat16 [8192, 512], P('tbl'), may hold values from -6 to 6
- w_up: bfloat16 [512, 4096], P(None, 'hst'), may hold values from -0.25 to 0.25
- grad_out: bfloat16 [8192, 4096], P('tbl', 'hst'), may hold values from -6 to 6
- owners: int32 [4, 8192, 8], P('hst', 'tbl'), may hold values from 0 to 15, all different within a row; in each aligned block of 512 rows (0 to 511, 512 to 1023, ..., all dimensions but the last counted through in order) at most 512 rows name the same one
- rows: int32 [4, 8192, 8], P('hst', 'tbl'), may hold values from 0 to 1023
- lookup_weight: bfloat16 [4, 8192, 8], P('hst', 'tbl'), may hold values from 0.25 to 2
- lens: int32 [4, 8192], P('hst', 'tbl'), may hold values from 4 to 8
- slot_map: int32 [16, 2, 2048], P('tbl', 'hst'), may hold values from 0 to 2047, each once within a row
- cache_weight: float32 [16, 2, 2048, 128], P('tbl', 'hst'), may hold values from -6 to 6
- cache_accum: float32 [16, 2, 2048], P('tbl', 'hst'), may hold values from 0.1 to 10
- evict_slots: int32 [16, 2, 256], P('tbl', 'hst'), may hold values from 0 to 2047, as said below
- evict_dest: int32 [16, 2, 256], P('tbl', 'hst'), may hold values from 0 to 1, as said below
- evict_count: int32 [16, 2], P('tbl', 'hst'), may hold values from 128 to 256
Outputs:
- grad_up: float32 [512, 4096], P('tbl', 'hst')
- new_weight: float32 [16, 2, 2048, 128], P('tbl', 'hst')
- new_accum: float32 [16, 2, 2048], P('tbl', 'hst')
- held_rows: float32 [16, 2, 2, 128, 128], P('tbl', 'hst')
- held_accum: float32 [16, 2, 2, 128], P('tbl', 'hst')
Inputs may be any that keep to these rules, and one draw needn't show every extreme that they name: The 8 owners of one bag differ. Among the 512 samples of one index of tbl and one table, no owner is named by more than 512 lookup positions, used or not; some owner is named by exactly 512 in some such block. `evict_slots`: the 256 slots of one device's list differ. `evict_dest`: among the used entries of one device, no holder appears more than 128 times, and one holder appears exactly 128 times.
All inputs are finite; a program needn't handle non-finite values.
Results may differ from a plain program's by a relative error of at most 0.0029.
Values may be sent and summed in bfloat16 or wider, within the bound.
A program may use at most 64 MiB of HBM per device.

v0:
```python
import functools

import jax
import jax.numpy as jnp
from jax import lax
from jax.experimental import pallas as pl
from jax.experimental.pallas import tpu as pltpu
from jax.sharding import PartitionSpec as P

LEARN_RATE = 0.05
EPSILON = 1e-08
MESH = pl.DeviceIdType.MESH
PIECES = 2
F32 = jnp.float32
BF16 = jnp.bfloat16


def exchange_kernel(
    nz, nx, nh, tables, rows_dev,
    feat, grad, idx,
    grad_out_ref, place_ref,
    ybuf, gat, idxb, rcore, a1, rx, a2, rz,
    y_s, y_r, i_s, i_r, azr_s, azl_s, ax_s, ac_s, g_r, rc_s, rc_r, rx_s, rx_r, rz_s, rz_r,
):
    n = nz * nx * 2
    me = lax.axis_index("tbl")
    h = lax.axis_index("hst")
    c = lax.rem(me, 2)
    zx = me // 2
    x = lax.rem(zx, nx)
    z = zx // nx
    other = 1 - c
    width = ybuf.shape[-1]
    emb = width // tables

    def at(zi, xi, ci):
        return (zi * nx + xi) * 2 + ci

    def zof(d):
        return lax.rem(z + d, nz)

    def xof(d):
        return lax.rem(x + d, nx)

    def rcopy(src, dst, s, r, dev):
        return pltpu.make_async_remote_copy(
            src_ref=src, dst_ref=dst, send_sem=s, recv_sem=r,
            device_id=dev, device_id_type=MESH,
        )

    barrier = pltpu.get_barrier_semaphore()

    def greet(d, carry):
        pl.semaphore_signal(
            barrier, inc=1, device_id={"tbl": lax.rem(me + d, n)}, device_id_type=MESH
        )
        return carry

    lax.fori_loop(1, n, greet, 0)
    for d in range(1, nh):
        pl.semaphore_signal(
            barrier, inc=1, device_id={"hst": lax.rem(h + d, nh)}, device_id_type=MESH
        )
    pl.semaphore_wait(barrier, n - 1 + nh - 1)

    def cols(hh):
        return pl.ds(pl.multiple_of(hh * width, width), width)

    batch = gat.shape[1]
    piece = batch // PIECES

    def span(k):
        return pl.ds(k * piece, piece)

    def y_copy(d, k):
        h2 = lax.rem(h + d, nh)
        return rcopy(
            feat.at[span(k), cols(h2)], ybuf.at[h, span(k)], y_s.at[d, k], y_r.at[h, k], {"hst": h2}
        )

    def y_arrival(d, k):
        h2 = lax.rem(h + d, nh)
        return rcopy(
            feat.at[span(k), cols(h2)], ybuf.at[h2, span(k)], y_s.at[d, k], y_r.at[h2, k],
            {"hst": h2},
        )

    def core_copy(x2):
        return rcopy(
            grad.at[:, x2, other], rcore.at[:, x2], rc_s.at[x2], rc_r.at[x2],
            {"tbl": at(z, x, other)},
        )

    def i_copy(d):
        o = lax.rem(me + d, n)
        return rcopy(idx.at[o], idxb.at[me], i_s.at[d], i_r.at[me], {"tbl": o})

    def i_arrival(slot):
        return rcopy(idx.at[slot], idxb.at[slot], i_s.at[0], i_r.at[slot], {"tbl": at(z, x, other)})

    for k in range(PIECES):
        for d in range(1, nh):
            y_copy(d, k).start()
    for d in range(1, nx + 1):
        core_copy(xof(d)).start()

    def i_start(d, carry):
        i_copy(d).start()
        return carry

    lax.fori_loop(1, n, i_start, 0)

    def rx_copy(d):
        x2 = xof(d)
        return rcopy(a1.at[:, x2], rx.at[x], rx_s.at[x2], rx_r.at[x], {"tbl": at(z, x2, c)})

    def rx_arrival(d):
        x2 = xof(d)
        return rcopy(a1.at[:, x2], rx.at[x2], rx_s.at[x2], rx_r.at[x2], {"tbl": at(z, x2, c)})

    for d in range(1, nx):
        x2 = xof(d)
        core_copy(x2).wait_recv()

        def add_core(k, carry):
            a1[k, x2] = (grad[k, x2, c] + rcore[k, x2]).astype(BF16)
            return carry

        lax.fori_loop(0, nz, add_core, 0)
        rx_copy(d).start()

    def g_copy(slot, k, sem, dev):
        ref = gat.at[slot, span(k)]
        return rcopy(ref, ref, sem, g_r.at[slot, k], {"tbl": dev})

    def right_copy(zi, k):
        return g_copy(at(zi, x, c), k, azr_s.at[zi, k], at(z + 1, x, c))

    def left_copy(zi, k):
        return g_copy(at(zi, x, c), k, azl_s.at[zi, k], at(z - 1, x, c))

    def x_copy(zi, d, k):
        return g_copy(at(zi, x, c), k, ax_s.at[zi, d, k], at(z, xof(d), c))

    def c_copy(zi, xi, k):
        return g_copy(at(zi, xi, c), k, ac_s.at[zi, xi, k], at(z, x, other))

    def arrived(slot, k):
        g_copy(slot, k, ac_s.at[0, 0, k], at(z, x, other)).wait_recv()

    for k in range(PIECES):
        for d in range(1, nh):
            y_arrival(d, k).wait_recv()
        total = feat[span(k), cols(h)].astype(F32)
        for d in range(1, nh):
            total = total + ybuf[lax.rem(h + d, nh), span(k)].astype(F32)
        gat[me, span(k)] = total.astype(BF16)

        @pl.when(z + 1 < nz)
        def _(k=k):
            right_copy(z, k).start()

        @pl.when(z >= 1)
        def _(k=k):
            left_copy(z, k).start()

        for d in range(1, nx):
            x_copy(z, d, k).start()
        c_copy(z, x, k).start()

    place_ref[...] = jnp.zeros_like(place_ref)
    idxb[me] = idx[me]
    chunk = min(256, rows_dev)

    def proc(slot):
        meta = idxb[slot]
        block = gat[slot]
        for t in range(tables):
            row = meta[t : t + 1, :]
            wgt = meta[tables + t : tables + t + 1, :]
            part = block[:, t * emb : (t + 1) * emb]
            for r0 in range(0, rows_dev, chunk):
                ids = lax.broadcasted_iota(jnp.int32, (chunk, batch), 0).astype(F32) + float(r0)
                mark = jnp.where(ids == row, wgt, 0.0).astype(BF16)
                place_ref[pl.ds(t * rows_dev + r0, chunk), :] += jnp.dot(
                    mark, part, preferred_element_type=F32
                )

    proc(me)

    def own_sum(k):
        s = grad[k, x, c] + rcore[k, x]
        for d in range(1, nx):
            s = s + rx[xof(d), k].astype(F32)
        return s

    def rz_copy(d):
        zi = zof(d)
        return rcopy(a2.at[zi], rz.at[z], rz_s.at[d], rz_r.at[z], {"tbl": at(zi, x, c)})

    def rz_arrival(d):
        zi = zof(d)
        return rcopy(a2.at[zi], rz.at[zi], rz_s.at[d], rz_r.at[zi], {"tbl": at(zi, x, c)})

    def rz_start(d, carry):
        zi = zof(d)
        a2[zi] = own_sum(zi).astype(BF16)
        rz_copy(d).start()
        return carry

    def from_z(zi, open_end, onward):
        slot = at(zi, x, c)
        for k in range(PIECES):
            arrived(slot, k)

            @pl.when(open_end)
            def _(k=k):
                onward(zi, k).start()

            for dx in range(1, nx):
                x_copy(zi, dx, k).start()
            c_copy(zi, x, k).start()
        i_arrival(slot).wait_recv()
        proc(slot)

    def from_x(zi):
        for dx in range(1, nx):
            slot = at(zi, xof(dx), c)
            for k in range(PIECES):
                arrived(slot, k)
                c_copy(zi, xof(dx), k).start()
            i_arrival(slot).wait_recv()
            proc(slot)

    def line_body(j, carry):
        @pl.when(z - j >= 0)
        def _():
            from_z(z - j, z + 1 < nz, right_copy)

        @pl.when(z + j < nz)
        def _():
            from_z(z + j, z >= 1, left_copy)

        @pl.when(j == (nz + 1) // 2)
        def _():
            core_copy(x).wait_recv()
            for d in range(1, nx):
                rx_arrival(d).wait_recv()
            lax.fori_loop(1, nz, rz_start, 0)

        @pl.when(z - j + 1 >= 0)
        def _():
            from_x(z - j + 1)

        @pl.when((j > 1) & (z + j - 1 < nz))
        def _():
            from_x(z + j - 1)

        return carry

    lax.fori_loop(1, nz + 1, line_body, 0)

    def c_body(k, carry):
        j = k // nz
        zi = zof(lax.rem(k, nz))
        slot = at(zi, xof(j), other)
        for p in range(PIECES):
            arrived(slot, p)
        i_arrival(slot).wait_recv()
        proc(slot)
        return carry

    lax.fori_loop(0, nz * nx, c_body, 0)

    grad_out_ref[...] = own_sum(z)

    def rz_end(d, carry):
        rz_arrival(d).wait_recv()
        grad_out_ref[...] += rz[zof(d)].astype(F32)
        return carry

    lax.fori_loop(1, nz, rz_end, 0)

    for p in range(PIECES):
        for d in range(1, nh):
            y_copy(d, p).wait_send()
    for d in range(1, nx + 1):
        core_copy(xof(d)).wait_send()
    for d in range(1, nx):
        rx_copy(d).wait_send()

    def i_end(d, carry):
        i_copy(d).wait_send()
        return carry

    lax.fori_loop(1, n, i_end, 0)

    def z_end(d, carry):
        rz_copy(d).wait_send()
        return carry

    lax.fori_loop(1, nz, z_end, 0)

    def end_all(k, carry):
        for p in range(PIECES):

            @pl.when((k <= z) & (z + 1 < nz))
            def _(p=p):
                right_copy(k, p).wait_send()

            @pl.when((k >= z) & (z >= 1))
            def _(p=p):
                left_copy(k, p).wait_send()

            for dx in range(1, nx):
                x_copy(k, dx, p).wait_send()
            for xi in range(nx):
                c_copy(k, xi, p).wait_send()
        return carry

    lax.fori_loop(0, nz, end_all, 0)


def update_kernel(
    slot_map, evict_slots, goal, place, weight, accum,
    new_weight, new_accum, send_rows, send_accum,
    sgrad, wide,
):
    slots = place.shape[0]
    list_len = evict_slots.shape[0]
    step = 16

    def scatter(i, carry):
        for j in range(step):
            r = i * step + j
            sgrad[pl.ds(slot_map[r], 1), :] = place[pl.ds(r, 1), :]
        return carry

    lax.fori_loop(0, slots // step, scatter, 0)
    tile = 128

    def adagrad(i, carry):
        at = pl.ds(i * tile, tile)
        g = sgrad[at, :]
        acc = accum[pl.ds(i, 1), :] + jnp.mean(g * g, axis=-1)[None, :]
        new_accum[pl.ds(i, 1), :] = acc
        col = jnp.broadcast_to(acc.reshape(tile, 1), g.shape)
        wide[at, :] = col
        new_weight[at, :] = weight[at, :] - LEARN_RATE * g / (jnp.sqrt(col) + EPSILON)
        return carry

    lax.fori_loop(0, slots // tile, adagrad, 0)
    send_rows[...] = jnp.zeros_like(send_rows)
    sgrad[...] = jnp.zeros_like(sgrad)

    def evict(i, carry):
        for j in range(8):
            p = i * 8 + j
            s = evict_slots[p]
            k = goal[p]
            send_rows[pl.ds(k, 1), :] = new_weight[pl.ds(s, 1), :]
            sgrad[pl.ds(k, 1), :] = wide[pl.ds(s, 1), :]
        return carry

    lax.fori_loop(0, list_len // 8, evict, 0)
    groups = send_accum.shape[0]
    cap = send_accum.shape[2]
    for d in range(groups):
        send_accum[d] = jnp.max(sgrad[d * cap : (d + 1) * cap, :], axis=-1)[None, :]


def hold_kernel(nh, rows, accum, held_rows, held_accum, rbuf, abuf, r_s, r_r, a_s, a_r):
    h = lax.axis_index("hst")
    cap = rbuf.shape[1]
    barrier = pltpu.get_barrier_semaphore()
    for d in range(1, nh):
        pl.semaphore_signal(
            barrier, inc=1, device_id={"hst": lax.rem(h + d, nh)}, device_id_type=MESH
        )
    pl.semaphore_wait(barrier, nh - 1)

    def part(k):
        return pl.ds(pl.multiple_of(k * cap, cap), cap)

    def copies(d, slot):
        k = lax.rem(h + d, nh)
        return [
            pltpu.make_async_remote_copy(
                src_ref=src, dst_ref=dst.at[slot], send_sem=s.at[d], recv_sem=r.at[slot],
                device_id={"hst": k}, device_id_type=MESH,
            )
            for src, dst, s, r in (
                (rows.at[part(k)], rbuf, r_s, r_r),
                (accum.at[k], abuf, a_s, a_r),
            )
        ]

    for d in range(1, nh):
        for copy in copies(d, h):
            copy.start()
    held_rows[h] = rows[part(h), :]
    held_accum[h] = accum[h]
    for d in range(1, nh):
        k = lax.rem(h + d, nh)
        for copy in copies(d, k):
            copy.wait_recv()
        held_rows[k] = rbuf[k]
        held_accum[k] = abuf[k]
    for d in range(1, nh):
        for copy in copies(d, h):
            copy.wait_send()


def on_device(
    nz, nx,
    pooled, w_up, grad_out, owners, rows, lookup_weight, lens, slot_map,
    cache_weight, cache_accum, evict_slots, evict_dest, evict_count,
):
    tables, batch, bag_len = owners.shape
    slots = slot_map.shape[-1]
    rows_dev = slots // tables
    emb = cache_weight.shape[-1]
    n = lax.axis_size("tbl")
    nh = lax.axis_size("hst")
    feat_n, hid = w_up.shape
    out_rows = feat_n // n
    width = tables * emb

    preact = jnp.dot(pooled, w_up, preferred_element_type=F32)
    sig = jax.nn.sigmoid(preact)
    delta = (grad_out.astype(F32) * sig * (1.0 + preact * (1.0 - sig))).astype(BF16)
    feat = lax.dot_general(
        delta, w_up, (((1,), (1,)), ((), ())), preferred_element_type=F32
    ).astype(BF16)
    grad = lax.dot_general(
        pooled, delta, (((0,), (0,)), ((), ())), preferred_element_type=F32
    )
    grad = grad.reshape(nz, nx, 2, out_rows, hid)

    own_t = jnp.transpose(owners, (2, 0, 1))
    row_t = jnp.transpose(rows, (2, 0, 1)).astype(F32)
    wgt_t = jnp.transpose(lookup_weight, (2, 0, 1)).astype(F32)
    used = jnp.arange(bag_len, dtype=jnp.int32)[:, None, None] < lens[None]
    hit = (own_t[None] == jnp.arange(n, dtype=jnp.int32)[:, None, None, None]) & used[None]
    row_to = jnp.sum(jnp.where(hit, row_t[None] + 1.0, 0.0), axis=1) - 1.0
    wgt_to = jnp.sum(jnp.where(hit, wgt_t[None], 0.0), axis=1)
    idx = jnp.concatenate([row_to, wgt_to], axis=1)

    dma = pltpu.SemaphoreType.DMA
    vmem = pl.BlockSpec(memory_space=pltpu.VMEM)
    smem = pl.BlockSpec(memory_space=pltpu.SMEM)
    grad_up, place = pl.pallas_call(
        functools.partial(exchange_kernel, nz, nx, nh, tables, rows_dev),
        out_shape=(
            jax.ShapeDtypeStruct((out_rows, hid), F32),
            jax.ShapeDtypeStruct((slots, emb), F32),
        ),
        in_specs=[vmem] * 3,
        out_specs=(vmem, vmem),
        scratch_shapes=[
            pltpu.VMEM((nh, batch, width), BF16),
            pltpu.VMEM((n, batch, width), BF16),
            pltpu.VMEM((n, 2 * tables, batch), F32),
            pltpu.VMEM((nz, nx, out_rows, hid), F32),
            pltpu.VMEM((nz, nx, out_rows, hid), BF16),
            pltpu.VMEM((nx, nz, out_rows, hid), BF16),
            pltpu.VMEM((nz, out_rows, hid), BF16),
            pltpu.VMEM((nz, out_rows, hid), BF16),
            dma((nh, PIECES)), dma((nh, PIECES)), dma((n,)), dma((n,)),
            dma((nz, PIECES)), dma((nz, PIECES)), dma((nz, nx, PIECES)), dma((nz, nx, PIECES)),
            dma((n, PIECES)),
            dma((nx,)), dma((nx,)), dma((nx,)), dma((nx,)), dma((nz,)), dma((nz,)),
        ],
        compiler_params=pltpu.CompilerParams(
            collective_id=0, has_side_effects=True, vmem_limit_bytes=60 * 1024 * 1024
        ),
        name="exchange",
    )(feat, grad, idx)

    chosen = evict_slots[0, 0]
    dest = evict_dest[0, 0]
    list_len = chosen.shape[0]
    cap = list_len // 2
    ids = jnp.arange(list_len, dtype=jnp.int32)
    live = ids < evict_count[0, 0]
    same = (dest[:, None] == dest[None, :]) & (ids[:, None] > ids[None, :]) & live[None, :]
    goal = jnp.where(live, dest * cap + jnp.sum(same.astype(jnp.int32), axis=1), nh * cap)

    new_weight, new_accum, send_rows, send_accum = pl.pallas_call(
        update_kernel,
        out_shape=(
            jax.ShapeDtypeStruct((slots, emb), F32),
            jax.ShapeDtypeStruct((slots // 128, 128), F32),
            jax.ShapeDtypeStruct((nh * cap + 8, emb), F32),
            jax.ShapeDtypeStruct((nh, 1, cap), F32),
        ),
        in_specs=[smem] * 3 + [vmem] * 3,
        out_specs=(vmem,) * 4,
        scratch_shapes=[pltpu.VMEM((slots, emb), F32), pltpu.VMEM((slots, emb), F32)],
        name="update",
    )(
        slot_map.reshape(slots), chosen, goal.astype(jnp.int32), place,
        cache_weight.reshape(slots, emb), cache_accum.reshape(slots // 128, 128),
    )
    held_rows, held_accum = pl.pallas_call(
        functools.partial(hold_kernel, nh),
        out_shape=(
            jax.ShapeDtypeStruct((nh, cap, emb), F32),
            jax.ShapeDtypeStruct((nh, 1, cap), F32),
        ),
        in_specs=[vmem, vmem],
        out_specs=(vmem, vmem),
        scratch_shapes=[
            pltpu.VMEM((nh, cap, emb), F32),
            pltpu.VMEM((nh, 1, cap), F32),
            dma((nh,)), dma((nh,)), dma((nh,)), dma((nh,)),
        ],
        compiler_params=pltpu.CompilerParams(collective_id=1, has_side_effects=True),
        name="hold",
    )(send_rows, send_accum)
    return (
        grad_up,
        new_weight[None, None],
        new_accum.reshape(1, 1, slots),
        held_rows[None, None],
        held_accum.reshape(1, 1, nh, cap),
    )


def solution(mesh):
    n, nh = mesh.shape["tbl"], mesh.shape["hst"]
    nx = nh if n % (2 * nh) == 0 else 1
    nz = n // (2 * nx)
    placed = (
        P("tbl", None),
        P(None, "hst"),
        P("tbl", "hst"),
        P("hst", "tbl", None),
        P("hst", "tbl", None),
        P("hst", "tbl", None),
        P("hst", "tbl"),
        P("tbl", "hst", None),
        P("tbl", "hst", None, None),
        P("tbl", "hst", None),
        P("tbl", "hst", None),
        P("tbl", "hst", None),
        P("tbl", "hst"),
    )
    return jax.shard_map(
        functools.partial(on_device, nz, nx),
        mesh=mesh,
        in_specs=placed,
        out_specs=(
            P("tbl", "hst"),
            P("tbl", "hst", None, None),
            P("tbl", "hst", None),
            P("tbl", "hst", None, None, None),
            P("tbl", "hst", None, None),
        ),
        check_vma=False,
    )
```

profile of v0, /device:TPU:0, one launch (start us, length us, event | category | flops | bytes accessed | tf_op | source)
XLA Modules:
  0.0 89.7 jit_solution(8206206735214477058)
XLA Ops:
  0.6 0.0 copy-start
  0.6 1.6 %copy-done = bf16[512,2048]{1,0:T(8,128)(2,1)S(1)} copy-done((bf16[512,2048]{1,0:T(8,128)(2,1)S(1)}, bf16[512,2048]{1,0:T(8,128)(2,1)}, u32[]{:S(2)}) %copy-start) | copy-done | bytes 2097176
  2.2 4.0 %multiply_convert_fusion = bf16[512,2048]{1,0:T(8,128)(2,1)S(1)} fusion(bf16[512,2048]{1,0:T(8,128)(2,1)} %param.15, bf16[512,512]{1,0:T(8,128)(2,1)} %param.13, bf16[512,2048]{1,0:T(8,128)(2,1)S(1)} %copy-done), kind=kOutput, calls=%fused_computation | convolution fusion | flops 1084227584 | bytes 6815744 | tf_op jit(solution)/shard_map/dot_general | solution.py:429
  6.3 0.0 copy-start.1
  6.3 2.1 %convolution_convert_fusion.feat = bf16[512,512]{1,0:T(8,128)(2,1)} fusion(bf16[512,2048]{1,0:T(8,128)(2,1)S(1)} %multiply_convert_fusion, bf16[512,2048]{1,0:T(8,128)(2,1)S(1)} %copy-done), kind=kOutput, calls=%fused_computation.1 | convolution fusion | flops 1074003968 | bytes 4718592 | tf_op jit(solution)/shard_map/dot_general | solution.py:432
  8.4 0.0 copy-done.1
  8.4 0.0 copy-start.3
  8.4 0.0 copy-start.7
  8.4 0.0 copy-start.5
  8.4 0.0 copy-start.4
  8.4 3.3 %fusion.3 = f32[2048,512]{0,1:T(8,128)} fusion(bf16[512,2048]{1,0:T(8,128)(2,1)S(1)} %multiply_convert_fusion, bf16[512,512]{1,0:T(8,128)(2,1)S(1)} %copy-done.1), kind=kOutput, calls=%fused_computation.17 | convolution fusion | flops 1073741824 | bytes 6815744 | tf_op jit(solution)/shard_map/dot_general | solution.py:435
  11.7 0.0 copy-done.3
  11.7 0.0 copy-done.7
  11.7 0.0 copy-done.5
  11.7 0.0 copy-done.4
  11.7 0.4 select_reduce_fusion.1
  12.2 0.7 pad_maximum_fusion.idx
  12.9 0.0 copy-start.6
  12.9 57.1 %exchange.1 = (f32[32,2048]{1,0:T(8,128)}, f32[2048,128]{1,0:T(8,128)}) custom-call(bf16[512,512]{1,0:T(8,128)(2,1)} %convolution_convert_fusion.feat, f32[4,2,2,32,2048]{4,3,2,1,0:T(8,128)} %bitcast.26, f32[16,4,512]{2,1,0:T(4,128)} %pad_maximum_fusion.idx), custom_call_target="tpu_custom_call" | custom-call | tf_op jit(solution)/shard_map/exchange/pallas_call | solution.py:452
  70.0 0.0 copy-start.2
  70.7 0.0 copy-done.6
  70.7 0.2 convert_reduce_fusion
  70.9 0.6 add_select_fusion.goal
  71.5 8.7 %update.1 = (f32[2048,128]{1,0:T(8,128)}, f32[16,128]{1,0:T(8,128)}, f32[264,128]{1,0:T(8,128)}, f32[2,1,128]{2,1,0:T(1,128)}) custom-call(s32[2048]{0:T(1024)} %bitcast.32, s32[256]{0:T(256)} %bitcast.34, s32[256]{0:T(256)} %add_select_fusion.goal, f32[2048,128]{1,0:T(8,128)} %get-tuple-element.14.place, f32[2048,128]{1,0:T(8,128)} %bitcast.27, ...), custom_call_target="tpu_custom_call" | custom-call | tf_op jit(solution)/shard_map/update/pallas_call | solution.py:489
  80.2 6.0 %hold.1 = (f32[2,128,128]{2,1,0:T(8,128)}, f32[2,1,128]{2,1,0:T(1,128)}) custom-call(f32[264,128]{1,0:T(8,128)} %get-tuple-element.17.rows, f32[2,1,128]{2,1,0:T(1,128)} %get-tuple-element.18.accum), custom_call_target="tpu_custom_call" | custom-call | tf_op jit(solution)/shard_map/hold/pallas_call | solution.py:505
  86.2 0.0 copy-done.2
  86.2 0.7 copy.25
  86.9 1.6 %copy.26 = f32[1,1,2,128,128]{4,3,2,1,0:T(8,128)} copy(f32[1,1,2,128,128]{4,3,2,1,0:T(8,128)} %bitcast.28) | data formatting | bytes 262144
  88.5 1.2 %copy.27 = f32[1,1,2,128]{3,2,1,0:T(2,128)} copy(f32[1,1,2,128]{3,2,1,0:T(2,128)} %bitcast.35) | data formatting | bytes 2048
  (5 shorter events, 0.1 us)
Async XLA Ops:
  0.6 1.6 %copy-start = (bf16[512,2048]{1,0:T(8,128)(2,1)S(1)}, bf16[512,2048]{1,0:T(8,128)(2,1)}, u32[]{:S(2)}) copy-start(bf16[512,2048]{1,0:T(8,128)(2,1)} %param.14) | copy-start | bytes 6291460
  6.3 2.1 %copy-start.1 = (bf16[512,512]{1,0:T(8,128)(2,1)S(1)}, bf16[512,512]{1,0:T(8,128)(2,1)}, u32[]{:S(2)}) copy-start(bf16[512,512]{1,0:T(8,128)(2,1)} %param.13) | copy-start | bytes 1572868
  8.4 3.3 %copy-start.3 = (s32[2,512,8]{1,2,0:T(8,128)S(1)}, s32[2,512,8]{1,2,0:T(8,128)}, u32[]{:S(2)}) copy-start(s32[2,512,8]{1,2,0:T(8,128)} %param.17) | copy-start | bytes 98308
  8.4 3.3 %copy-start.7 = (s32[2,512]{1,0:T(2,128)S(1)}, s32[2,512]{1,0:T(2,128)}, u32[]{:S(2)}) copy-start(s32[2,512]{1,0:T(2,128)} %param.19) | copy-start | bytes 12292
  8.4 3.3 %copy-start.5 = (bf16[2,512,8]{1,2,0:T(8,128)(2,1)S(1)}, bf16[2,512,8]{1,2,0:T(8,128)(2,1)}, u32[]{:S(2)}) copy-start(bf16[2,512,8]{1,2,0:T(8,128)(2,1)} %param.18) | copy-start | bytes 49156
  8.4 3.3 %copy-start.4 = (s32[2,512,8]{1,2,0:T(8,128)S(1)}, s32[2,512,8]{1,2,0:T(8,128)}, u32[]{:S(2)}) copy-start(s32[2,512,8]{1,2,0:T(8,128)} %param.16) | copy-start | bytes 98308
  12.9 57.8 %copy-start.6 = (s32[1,1,256]{2,1,0:T(1,128)S(1)}, s32[1,1,256]{2,1,0:T(1,128)}, u32[]{:S(2)}) copy-start(s32[1,1,256]{2,1,0:T(1,128)} %param.24) | copy-start | bytes 3076
  70.0 16.2 %copy-start.2 = (f32[32,2048]{1,0:T(8,128)S(1)}, f32[32,2048]{1,0:T(8,128)}, u32[]{:S(2)}) copy-start(f32[32,2048]{1,0:T(8,128)} %get-tuple-element.28) | copy-start | bytes 786436
where the time goes:
time: 90 us; the launch traced here: 89.7 us
  Pallas kernels  71.8 us (80%)
  matrix products  9.38 us (10%)
  local copies, waits for them, and re-layouts  5.12 us (6%)
  other arithmetic  1.94 us (2%)
  between operations  1.46 us (2%)
    pallas_call x1, Pallas kernels, on_device(): pl.pallas_call(functools.partial(exchange_kernel, nz, nx, nh, tables, row...  57.1 us
    pallas_call x1, Pallas kernels, on_device(): pl.pallas_call(update_kernel, out_shape=(jax.ShapeDtypeStruct((slots, emb...  8.71 us
    pallas_call x1, Pallas kernels, on_device(): pl.pallas_call(functools.partial(hold_kernel, nh), out_shape=(jax.ShapeDt...  5.99 us
    unnamed x19, local copies, waits for them, and re-layouts  5.12 us
    dot_general x1, matrix products, on_device(): preact = jnp.dot(pooled, w_up, preferred_element_type=F32)  4.03 us
    dot_general x1, matrix products, on_device(): lax.dot_general(pooled, delta, (((0,), (0,)), ((), ())), preferred_elemen...  3.26 us
    dot_general x1, matrix products, on_device(): lax.dot_general(delta, w_up, (((1,), (1,)), ((), ())), preferred_element_...  2.09 us

commit v1 on v0

v1 whole, which is shorter than its diff:
```python
import functools

import jax
import jax.numpy as jnp
from jax import lax
from jax.experimental import pallas as pl
from jax.experimental.pallas import tpu as pltpu
from jax.sharding import PartitionSpec as P

LEARN_RATE = 0.05
EPSILON = 1e-08
MESH = pl.DeviceIdType.MESH
BLOCKS = 2
SUBS = 2
PIECES = BLOCKS * SUBS
CUTS = 4
RADIX = 256
ROW_STEP = 2048.0
WEIGHT_STEP = 512.0
F32 = jnp.float32
BF16 = jnp.bfloat16
NT_DIMS = (((1,), (1,)), ((), ()))


def iota(shape, axis):
    return lax.broadcasted_iota(jnp.int32, shape, axis)


def step_kernel(
    nz, nx, nh, tables, rows_dev, tile,
    pooled, w_up, grad_out, owners, rows, lookup_weight, lens, slot_map,
    weight, accum, evict_slots, evict_dest, evict_count,
    grad_up, new_weight, new_accum, held_rows, held_accum,
    pooled_v, pooled_t, w_v, go_v, delta, own_v, row_v, lw_v, len_v, map_v, weight_v, accum_v,
    es_v, ed_v, ec_v,
    fown, fsend, ybuf, gat, idx, idxb, grad, rcore, chain, rin, lin, xs, xr, place,
    wide, inv_v, src_v, inv_s, src_s, ev_w, ev_a, ev_g, ev_rows, ev_acc, rows_in, acc_in,
    ld_s, sm_s, y_s, y_r, i_s, i_r, azr_s, azl_s, ax_s, ac_s, g_r, rc_s, rc_r,
    ch_s, rin_r, lin_r, xs_s, xr_r, er_s, er_r, ea_s, ea_r,
):
    n = nz * nx * 2
    me = lax.axis_index("tbl")
    h = lax.axis_index("hst")
    c = lax.rem(me, 2)
    zx = me // 2
    x = lax.rem(zx, nx)
    z = zx // nx
    other = 1 - c
    batch, hid = grad_out.shape
    feat_n = pooled.shape[1]
    width = ybuf.shape[-1]
    emb = width // tables
    bag = owners.shape[1]
    slots = weight.shape[0]
    list_len = evict_slots.shape[1]
    cap = ev_rows.shape[1]
    out_rows = grad.shape[4]
    cut = hid // CUTS
    piece = batch // PIECES
    block = batch // BLOCKS
    tiles = hid // tile

    def at(zi, xi, ci):
        return (zi * nx + xi) * 2 + ci

    def xof(d):
        return lax.rem(x + d, nx)

    def rcopy(src, dst, s, r, dev):
        return pltpu.make_async_remote_copy(
            src_ref=src, dst_ref=dst, send_sem=s, recv_sem=r,
            device_id=dev, device_id_type=MESH,
        )

    def cols(hh):
        return pl.ds(pl.multiple_of(hh * width, width), width)

    def span(k):
        return pl.ds(k * piece, piece)

    def spanb(k):
        return pl.ds(k * block, block)

    def cutcols(j):
        return pl.ds(j * cut, cut)

    loads = [pltpu.make_async_copy(pooled, pooled_v, ld_s.at[0])]
    w_loads = [
        pltpu.make_async_copy(
            w_up.at[:, pl.ds(j * tile, tile)], w_v.at[:, pl.ds(j * tile, tile)], ld_s.at[1 + j]
        )
        for j in range(tiles)
    ]
    g_loads = [
        pltpu.make_async_copy(grad_out.at[spanb(k)], go_v.at[spanb(k)], ld_s.at[1 + tiles + k])
        for k in range(BLOCKS)
    ]
    base = 1 + tiles + BLOCKS
    small = [
        pltpu.make_async_copy(src, dst, ld_s.at[base + k])
        for k, (src, dst) in enumerate((
            (owners, own_v), (rows, row_v), (lookup_weight, lw_v), (lens, len_v),
            (slot_map, map_v), (evict_slots, es_v), (evict_dest, ed_v), (evict_count, ec_v),
            (accum, accum_v), (weight, weight_v),
        ))
    ]
    loads[0].start()
    w_loads[0].start()
    g_loads[0].start()
    for copy in w_loads[1:] + g_loads[1:] + small:
        copy.start()

    barrier = pltpu.get_barrier_semaphore()

    def greet(d, carry):
        pl.semaphore_signal(
            barrier, inc=1, device_id={"tbl": lax.rem(me + d, n)}, device_id_type=MESH
        )
        return carry

    lax.fori_loop(1, n, greet, 0)
    for d in range(1, nh):
        pl.semaphore_signal(
            barrier, inc=1, device_id={"hst": lax.rem(h + d, nh)}, device_id_type=MESH
        )

    def y_copy(d, k):
        h2 = lax.rem(h + d, nh)
        return rcopy(
            fsend.at[d - 1, span(k)], ybuf.at[h, span(k)], y_s.at[d, k], y_r.at[h, k], {"hst": h2}
        )

    def y_arrival(d, k):
        h2 = lax.rem(h + d, nh)
        return rcopy(
            fsend.at[d - 1, span(k)], ybuf.at[h2, span(k)], y_s.at[d, k], y_r.at[h2, k],
            {"hst": h2},
        )

    def deltas(k):
        g_loads[k].wait()
        for j in range(tiles):
            if k == 0:
                w_loads[j].wait()
            cs = pl.ds(j * tile, tile)
            p = jnp.dot(pooled_v[spanb(k), :], w_v[:, cs], preferred_element_type=F32)
            s = jax.nn.sigmoid(p)
            g = go_v[spanb(k), cs].astype(F32)
            delta[spanb(k), cs] = (g * s * (1.0 + p * (1.0 - s))).astype(BF16)

    def feats(k):
        for d in range(1, nh):
            h2 = lax.rem(h + d, nh)
            part = lax.dot_general(
                delta[spanb(k), :], w_v[cols(h2), :], NT_DIMS, preferred_element_type=F32
            )
            fsend[d - 1, spanb(k)] = part.astype(BF16)
            for q in range(SUBS):
                y_copy(d, k * SUBS + q).start()
        fown[spanb(k), :] = lax.dot_general(
            delta[spanb(k), :], w_v[cols(h), :], NT_DIMS, preferred_element_type=F32
        )

    loads[0].wait()
    deltas(0)
    pl.semaphore_wait(barrier, n - 1 + nh - 1)
    feats(0)
    deltas(1)
    feats(1)

    def g_copy(slot, k, sem, dev):
        ref = gat.at[slot, span(k)]
        return rcopy(ref, ref, sem, g_r.at[slot, k], {"tbl": dev})

    def right_copy(zi, k):
        return g_copy(at(zi, x, c), k, azr_s.at[zi, k], at(z + 1, x, c))

    def left_copy(zi, k):
        return g_copy(at(zi, x, c), k, azl_s.at[zi, k], at(z - 1, x, c))

    def x_copy(zi, d, k):
        return g_copy(at(zi, x, c), k, ax_s.at[zi, d, k], at(z, xof(d), c))

    def c_copy(zi, xi, k):
        return g_copy(at(zi, xi, c), k, ac_s.at[zi, xi, k], at(z, x, other))

    def arrived(slot, k):
        g_copy(slot, k, ac_s.at[0, 0, k], at(z, x, other)).wait_recv()

    def gather_start(k):
        total = fown[span(k), :]
        for d in range(1, nh):
            y_arrival(d, k).wait_recv()
            total = total + ybuf[lax.rem(h + d, nh), span(k)].astype(F32)
        gat[me, span(k)] = total.astype(BF16)

        @pl.when(z + 1 < nz)
        def _():
            right_copy(z, k).start()

        @pl.when(z >= 1)
        def _():
            left_copy(z, k).start()

        for d in range(1, nx):
            x_copy(z, d, k).start()
        c_copy(z, x, k).start()

    def core_copy(j):
        return rcopy(
            grad.at[j, :, :, other], rcore.at[j], rc_s.at[j], rc_r.at[j], {"tbl": at(z, x, other)}
        )

    def weight_grad(j):
        part = jnp.dot(pooled_t[...], delta[:, cutcols(j)], preferred_element_type=F32)
        grad[j] = part.reshape(nz, nx, 2, out_rows, cut)
        core_copy(j).start()

    def i_copy(d):
        o = lax.rem(me + d, n)
        return rcopy(idx.at[o], idxb.at[me], i_s.at[d], i_r.at[me], {"tbl": o})

    def i_arrival(slot):
        return rcopy(idx.at[slot], idxb.at[slot], i_s.at[0], i_r.at[slot], {"tbl": at(z, x, other)})

    for copy in small:
        copy.wait()
    for t in range(tables):
        used = iota((bag, batch), 0) < len_v[t : t + 1, :]
        code = (row_v[t] + 1).astype(F32) * ROW_STEP + lw_v[t].astype(F32) * WEIGHT_STEP
        code = jnp.where(used, code, 0.0)
        for o in range(n):
            idx[o, t : t + 1, :] = jnp.sum(
                jnp.where(own_v[t] == o, code, 0.0), axis=0, keepdims=True
            )
    idxb[me] = idx[me]

    def i_start(d, carry):
        i_copy(d).start()
        return carry

    lax.fori_loop(1, n, i_start, 0)
    pooled_t[...] = pooled_v[...].T

    for k in range(PIECES):
        gather_start(k)
        for j in range(k * CUTS // PIECES, (k + 1) * CUTS // PIECES):
            weight_grad(j)

    place[...] = jnp.zeros_like(place)
    chunk = min(RADIX, rows_dev)

    def proc(slot):
        codes = idxb[slot]
        bags = gat[slot]
        for t in range(tables):
            code = codes[t : t + 1, :]
            row1 = jnp.floor(code * (1.0 / ROW_STEP))
            wgt = (code - row1 * ROW_STEP) * (1.0 / WEIGHT_STEP)
            row = row1 - 1.0
            part = bags[:, t * emb : (t + 1) * emb]
            for r0 in range(0, rows_dev, chunk):
                ids = iota((chunk, batch), 0).astype(F32) + float(r0)
                mark = jnp.where(ids == row, wgt, 0.0).astype(BF16)
                place[pl.ds(t * rows_dev + r0, chunk), :] += jnp.dot(
                    mark, part, preferred_element_type=F32
                )

    proc(me)

    eye = iota((emb, emb), 0) == iota((emb, emb), 1)
    groups = slots // emb

    def widen(i, carry):
        col = jnp.sum(jnp.where(eye, accum_v[pl.ds(i, 1), :], 0.0), axis=1, keepdims=True)
        wide[pl.ds(i * emb, emb), :] = jnp.broadcast_to(col, (emb, emb))
        return carry

    lax.fori_loop(0, groups, widen, 0)
    home = map_v[...].astype(F32)
    high = jnp.floor(home * (1.0 / emb))
    low = home - high * emb
    from_row = iota((1, slots), 1).astype(F32)
    from_high = jnp.floor(from_row * (1.0 / RADIX))
    from_low = from_row - from_high * RADIX
    in_group = iota((groups, slots), 0).astype(F32) == high
    left = jnp.concatenate(
        [jnp.where(in_group, from_high, 0.0), jnp.where(in_group, from_low, 0.0)], axis=0
    ).astype(BF16)
    right = jnp.where(iota((emb, slots), 0).astype(F32) == low, 1.0, 0.0).astype(BF16)
    found = lax.dot_general(left, right, NT_DIMS, preferred_element_type=F32)
    inv = (found[:groups] * RADIX + found[groups:]).astype(jnp.int32)
    inv_v[...] = jnp.clip(inv, 0, slots - 1)
    inv_copy = pltpu.make_async_copy(inv_v, inv_s, sm_s.at[0])
    inv_copy.start()

    live = iota((1, list_len), 1) < ec_v[...]
    lanes = 8 * -(-nh // 8)
    mine = jnp.where((iota((lanes, list_len), 0) == ed_v[...]) & live, 1.0, 0.0)
    before = jnp.where(iota((list_len, list_len), 0) < iota((list_len, list_len), 1), 1.0, 0.0)
    goal = jnp.dot(mine.astype(BF16), before.astype(BF16), preferred_element_type=F32)
    slot1 = es_v[...].astype(F32) + 1.0
    slot_high = jnp.floor(slot1 * (1.0 / RADIX))
    slot_low = slot1 - slot_high * RADIX
    parts = jnp.where(iota((8, list_len), 0) == 0, slot_high, slot_low).astype(BF16)
    for d in range(nh):
        hot = jnp.where(
            iota((cap, list_len), 0).astype(F32) == goal[d : d + 1], mine[d : d + 1], 0.0
        ).astype(BF16)
        got = lax.dot_general(parts, hot, NT_DIMS, preferred_element_type=F32)
        src = (got[0:1] * RADIX + got[1:2]).astype(jnp.int32)
        src_v[d : d + 1, :] = jnp.clip(src, 0, slots)
    src_copy = pltpu.make_async_copy(src_v, src_s, sm_s.at[1])
    src_copy.start()
    inv_copy.wait()
    src_copy.wait()

    def slot_of(k, p):
        s1 = src_s[k, p]
        return s1 > 0, jnp.maximum(s1 - 1, 0)

    def ev_fetch(i, carry):
        k = i // (cap // 8)
        p = lax.rem(i, cap // 8) * 8
        for q in range(8):
            ok, s = slot_of(k, p + q)
            ev_w[k, pl.ds(p + q, 1), :] = jnp.where(ok, weight_v[pl.ds(s, 1), :], 0.0)
            ev_a[k, pl.ds(p + q, 1), :] = jnp.where(ok, wide[pl.ds(s, 1), :], 0.0)
        return carry

    lax.fori_loop(0, nh * cap // 8, ev_fetch, 0)

    def rin_copy(t, j):
        return rcopy(
            chain.at[t, j], rin.at[t, j], ch_s.at[t, j], rin_r.at[t, j], {"tbl": at(z + 1, x, c)}
        )

    def lin_copy(t, j):
        return rcopy(
            chain.at[t, j], lin.at[t, j], ch_s.at[t, j], lin_r.at[t, j], {"tbl": at(z - 1, x, c)}
        )

    def own_sum(t, j, xi):
        return grad[j, t, xi, c] + rcore[j, t, xi]

    def chain_step(t, j, buf, copy):
        for xi in range(nx):
            s = own_sum(t, j, xi)
            if buf is not None:
                s = s + buf[t, j, xi].astype(F32)
            chain[t, j, xi] = s.astype(BF16)
        copy(t, j).start()

    for j in range(CUTS):
        core_copy(j).wait_recv()

    @pl.when(z == 0)
    def _():
        def body(i, carry):
            for j in range(CUTS):
                chain_step(nz - 1 - i, j, None, rin_copy)
            return carry

        lax.fori_loop(0, nz - 1, body, 0)

    @pl.when(z == nz - 1)
    def _():
        def body(i, carry):
            for j in range(CUTS):
                chain_step(i, j, None, lin_copy)
            return carry

        lax.fori_loop(0, nz - 1, body, 0)

    def from_z(zi, open_end, onward):
        slot = at(zi, x, c)
        for k in range(PIECES):
            arrived(slot, k)

            @pl.when(open_end)
            def _(k=k):
                onward(zi, k).start()

            for dx in range(1, nx):
                x_copy(zi, dx, k).start()
            c_copy(zi, x, k).start()

    def own_proc(slot):
        i_arrival(slot).wait_recv()
        proc(slot)

    def from_x(zi):
        for dx in range(1, nx):
            slot = at(zi, xof(dx), c)
            for k in range(PIECES):
                arrived(slot, k)
                c_copy(zi, xof(dx), k).start()
            own_proc(slot)

    def from_core(zi, xi):
        slot = at(zi, xi, other)
        for k in range(PIECES):
            arrived(slot, k)
        own_proc(slot)

    def from_core_x(zi):
        for dx in range(1, nx):
            from_core(zi, xof(dx))

    zr = nz - 1 - z

    def line_body(j, carry):
        below, above = z - j >= 0, z + j < nz

        @pl.when(below)
        def _():
            from_z(z - j, z + 1 < nz, right_copy)

        @pl.when(above)
        def _():
            from_z(z + j, z >= 1, left_copy)

        s = j - 1

        @pl.when((s <= nz - 2) & (z >= 1) & (z <= s))
        def _():
            t = nz - 1 - s + z
            for q in range(CUTS):
                rin_copy(t, q).wait_recv()
                chain_step(t, q, rin, rin_copy)

        @pl.when((s <= nz - 2) & (zr >= 1) & (zr <= s))
        def _():
            t = s - zr
            for q in range(CUTS):
                lin_copy(t, q).wait_recv()
                chain_step(t, q, lin, lin_copy)

        @pl.when(below)
        def _():
            own_proc(at(z - j, x, c))

        @pl.when(above)
        def _():
            own_proc(at(z + j, x, c))

        @pl.when(z - s >= 0)
        def _():
            from_x(z - s)
            from_core(z - s, x)

        @pl.when((s >= 1) & (z + s < nz))
        def _():
            from_x(z + s)
            from_core(z + s, x)

        @pl.when((s >= 1) & (z - s + 1 >= 0))
        def _():
            from_core_x(z - s + 1)

        @pl.when((s >= 2) & (z + s - 1 < nz))
        def _():
            from_core_x(z + s - 1)

        return carry

    lax.fori_loop(1, nz + 1, line_body, 0)

    def xs_copy(d, j):
        x2 = xof(d)
        return rcopy(xs.at[d - 1, j], xr.at[x, j], xs_s.at[d, j], xr_r.at[x, j], {"tbl": at(z, x2, c)})

    def xs_arrival(d, j):
        x2 = xof(d)
        return rcopy(xs.at[d - 1, j], xr.at[x2, j], xs_s.at[d, j], xr_r.at[x2, j], {"tbl": at(z, x2, c)})

    @pl.when(z >= 1)
    def _():
        for j in range(CUTS):
            rin_copy(z, j).wait_recv()
            for xi in range(nx):
                grad[j, z, xi, c] += rin[z, j, xi].astype(F32)

    @pl.when(z + 1 < nz)
    def _():
        for j in range(CUTS):
            lin_copy(z, j).wait_recv()
            for xi in range(nx):
                grad[j, z, xi, c] += lin[z, j, xi].astype(F32)

    for j in range(CUTS):
        for d in range(1, nx):
            xs[d - 1, j] = own_sum(z, j, xof(d)).astype(BF16)
            xs_copy(d, j).start()

    @pl.when(z == 0)
    def _():
        from_core_x(nz - 1)

    @pl.when(z == nz - 1)
    def _():
        from_core_x(0)

    def gathered(first):
        picks = []
        for q in range(8):
            picks.append(place[pl.ds(first(q), 1), :])
        return jnp.concatenate(picks, axis=0)

    def row_of(s):
        return inv_s[s // emb, lax.rem(s, emb)]

    def ev_gather(i, carry):
        k = i // (cap // 8)
        p = lax.rem(i, cap // 8) * 8
        for q in range(8):
            ok, s = slot_of(k, p + q)
            ev_g[k, pl.ds(p + q, 1), :] = jnp.where(ok, place[pl.ds(row_of(s), 1), :], 0.0)
        return carry

    lax.fori_loop(0, nh * cap // 8, ev_gather, 0)

    def er_copy(d, slot):
        k = lax.rem(h + d, nh)
        return rcopy(ev_rows.at[k], rows_in.at[slot], er_s.at[d], er_r.at[slot], {"hst": k})

    def ea_copy(d, slot):
        k = lax.rem(h + d, nh)
        return rcopy(ev_acc.at[k], acc_in.at[slot], ea_s.at[d], ea_r.at[slot], {"hst": k})

    for d in range(1, nh + 1):
        k = lax.rem(h + d, nh)
        for r0 in range(0, cap, emb):
            span_k = pl.ds(r0, emb)
            g = ev_g[k, span_k]
            acc = ev_a[k, span_k] + jnp.mean(g * g, axis=1, keepdims=True)
            ev_rows[k, span_k] = ev_w[k, span_k] - LEARN_RATE * g / (jnp.sqrt(acc) + EPSILON)
            ev_acc[k, :, span_k] = jnp.sum(jnp.where(eye, acc, 0.0), axis=0, keepdims=True)
        if d < nh:
            er_copy(d, h).start()
            ea_copy(d, h).start()
    held_rows[h] = ev_rows[h]
    held_accum[h] = ev_acc[h]

    def update(i, carry):
        total = jnp.zeros((8, emb), F32)
        for b in range(emb // 8):
            rows_b = pl.ds(pl.multiple_of(i * emb + b * 8, 8), 8)
            g = gathered(lambda q: inv_s[i, b * 8 + q])
            acc = wide[rows_b, :] + jnp.mean(g * g, axis=1, keepdims=True)
            new_weight[rows_b, :] = weight_v[rows_b, :] - LEARN_RATE * g / (
                jnp.sqrt(acc) + EPSILON
            )
            diag = iota((8, emb), 1) == iota((8, emb), 0) + b * 8
            total = total + jnp.where(diag, acc, 0.0)
        new_accum[pl.ds(i, 1), :] = jnp.sum(total, axis=0, keepdims=True)
        return carry

    lax.fori_loop(0, groups, update, 0)

    for j in range(CUTS):
        s = own_sum(z, j, x)
        for d in range(1, nx):
            xs_arrival(d, j).wait_recv()
            s = s + xr[xof(d), j].astype(F32)
        grad_up[:, cutcols(j)] = s

    for d in range(1, nh):
        k = lax.rem(h + d, nh)
        er_copy(d, k).wait_recv()
        ea_copy(d, k).wait_recv()
        held_rows[k] = rows_in[k]
        held_accum[k] = acc_in[k]

    for d in range(1, nh):
        er_copy(d, h).wait_send()
        ea_copy(d, h).wait_send()
        for k in range(PIECES):
            y_copy(d, k).wait_send()
    for j in range(CUTS):
        core_copy(j).wait_send()
        for d in range(1, nx):
            xs_copy(d, j).wait_send()

    def i_end(d, carry):
        i_copy(d).wait_send()
        return carry

    lax.fori_loop(1, n, i_end, 0)

    def end_all(k, carry):
        @pl.when(k > z)
        def _():
            for j in range(CUTS):
                rin_copy(k, j).wait_send()

        @pl.when(k < z)
        def _():
            for j in range(CUTS):
                lin_copy(k, j).wait_send()

        for p in range(PIECES):

            @pl.when((k <= z) & (z + 1 < nz))
            def _(p=p):
                right_copy(k, p).wait_send()

            @pl.when((k >= z) & (z >= 1))
            def _(p=p):
                left_copy(k, p).wait_send()

            for dx in range(1, nx):
                x_copy(k, dx, p).wait_send()
            for xi in range(nx):
                c_copy(k, xi, p).wait_send()
        return carry

    lax.fori_loop(0, nz, end_all, 0)


def on_device(
    nz, nx,
    pooled, w_up, grad_out, owners, rows, lookup_weight, lens, slot_map,
    cache_weight, cache_accum, evict_slots, evict_dest, evict_count,
):
    tables, batch, bag = owners.shape
    slots = slot_map.shape[-1]
    rows_dev = slots // tables
    emb = cache_weight.shape[-1]
    n = lax.axis_size("tbl")
    nh = lax.axis_size("hst")
    feat_n, hid = w_up.shape
    out_rows = feat_n // n
    width = tables * emb
    groups = slots // emb
    list_len = evict_slots.shape[-1]
    cap = list_len // 2
    cut = hid // CUTS
    tile = min(512, hid)

    dma = pltpu.SemaphoreType.DMA
    vmem = pl.BlockSpec(memory_space=pltpu.VMEM)
    anyspace = pl.BlockSpec(memory_space=pl.ANY)
    i32 = jnp.int32
    grad_up, new_weight, new_accum, held_rows, held_accum = pl.pallas_call(
        functools.partial(step_kernel, nz, nx, nh, tables, rows_dev, tile),
        out_shape=(
            jax.ShapeDtypeStruct((out_rows, hid), F32),
            jax.ShapeDtypeStruct((slots, emb), F32),
            jax.ShapeDtypeStruct((groups, emb), F32),
            jax.ShapeDtypeStruct((nh, cap, emb), F32),
            jax.ShapeDtypeStruct((nh, 1, cap), F32),
        ),
        in_specs=[anyspace] * 13,
        out_specs=(vmem,) * 5,
        scratch_shapes=[
            pltpu.VMEM((batch, feat_n), BF16),
            pltpu.VMEM((feat_n, batch), BF16),
            pltpu.VMEM((feat_n, hid), BF16),
            pltpu.VMEM((batch, hid), BF16),
            pltpu.VMEM((batch, hid), BF16),
            pltpu.VMEM((tables, bag, batch), i32),
            pltpu.VMEM((tables, bag, batch), i32),
            pltpu.VMEM((tables, bag, batch), BF16),
            pltpu.VMEM((tables, batch), i32),
            pltpu.VMEM((1, slots), i32),
            pltpu.VMEM((slots, emb), F32),
            pltpu.VMEM((groups, emb), F32),
            pltpu.VMEM((1, list_len), i32),
            pltpu.VMEM((1, list_len), i32),
            pltpu.VMEM((1, 1), i32),
            pltpu.VMEM((batch, width), F32),
            pltpu.VMEM((nh - 1, batch, width), BF16),
            pltpu.VMEM((nh, batch, width), BF16),
            pltpu.VMEM((n, batch, width), BF16),
            pltpu.VMEM((n, tables, batch), F32),
            pltpu.VMEM((n, tables, batch), F32),
            pltpu.VMEM((CUTS, nz, nx, 2, out_rows, cut), F32),
            pltpu.VMEM((CUTS, nz, nx, out_rows, cut), F32),
            pltpu.VMEM((nz, CUTS, nx, out_rows, cut), BF16),
            pltpu.VMEM((nz, CUTS, nx, out_rows, cut), BF16),
            pltpu.VMEM((nz, CUTS, nx, out_rows, cut), BF16),
            pltpu.VMEM((max(nx - 1, 1), CUTS, out_rows, cut), BF16),
            pltpu.VMEM((nx, CUTS, out_rows, cut), BF16),
            pltpu.VMEM((slots, emb), F32),
            pltpu.VMEM((slots, emb), F32),
            pltpu.VMEM((groups, emb), i32),
            pltpu.VMEM((nh, cap), i32),
            pltpu.SMEM((groups, emb), i32),
            pltpu.SMEM((nh, cap), i32),
            pltpu.VMEM((nh, cap, emb), F32),
            pltpu.VMEM((nh, cap, emb), F32),
            pltpu.VMEM((nh, cap, emb), F32),
            pltpu.VMEM((nh, cap, emb), F32),
            pltpu.VMEM((nh, 1, cap), F32),
            pltpu.VMEM((nh, cap, emb), F32),
            pltpu.VMEM((nh, 1, cap), F32),
            dma((1 + hid // tile + BLOCKS + 10,)), dma((2,)),
            dma((nh, PIECES)), dma((nh, PIECES)), dma((n,)), dma((n,)),
            dma((nz, PIECES)), dma((nz, PIECES)), dma((nz, nx, PIECES)), dma((nz, nx, PIECES)),
            dma((n, PIECES)), dma((CUTS,)), dma((CUTS,)),
            dma((nz, CUTS)), dma((nz, CUTS)), dma((nz, CUTS)),
            dma((nx, CUTS)), dma((nx, CUTS)),
            dma((nh,)), dma((nh,)), dma((nh,)), dma((nh,)),
        ],
        compiler_params=pltpu.CompilerParams(
            collective_id=0, has_side_effects=True, vmem_limit_bytes=56 * 1024 * 1024
        ),
        name="step",
    )(
        pooled, w_up, grad_out,
        jnp.transpose(owners, (0, 2, 1)), jnp.transpose(rows, (0, 2, 1)),
        jnp.transpose(lookup_weight, (0, 2, 1)), lens, slot_map.reshape(1, slots),
        cache_weight.reshape(slots, emb), cache_accum.reshape(groups, emb),
        evict_slots.reshape(1, list_len), evict_dest.reshape(1, list_len), evict_count,
    )
    return (
        grad_up,
        new_weight[None, None],
        new_accum.reshape(1, 1, slots),
        held_rows[None, None],
        held_accum.reshape(1, 1, nh, cap),
    )


def solution(mesh):
    n, nh = mesh.shape["tbl"], mesh.shape["hst"]
    nx = nh if n % (2 * nh) == 0 else 1
    nz = n // (2 * nx)
    placed = (
        P("tbl", None),
        P(None, "hst"),
        P("tbl", "hst"),
        P("hst", "tbl", None),
        P("hst", "tbl", None),
        P("hst", "tbl", None),
        P("hst", "tbl"),
        P("tbl", "hst", None),
        P("tbl", "hst", None, None),
        P("tbl", "hst", None),
        P("tbl", "hst", None),
        P("tbl", "hst", None),
        P("tbl", "hst"),
    )
    return jax.shard_map(
        functools.partial(on_device, nz, nx),
        mesh=mesh,
        in_specs=placed,
        out_specs=(
            P("tbl", "hst"),
            P("tbl", "hst", None, None),
            P("tbl", "hst", None),
            P("tbl", "hst", None, None, None),
            P("tbl", "hst", None, None),
        ),
        check_vma=False,
    )
```

time: 90 us -> 58.9 us (0.65)
  Pallas kernels: 71.8 us -> 51.6 us
  matrix products: 9.38 us -> 0 us
  other arithmetic: 1.94 us -> 0 us
    pallas_call x3 -> x1, Pallas kernels: 71.8 us -> 51.6 us  [on_device(): pl.pallas_call(functools.partial(step_kernel, nz, nx, nh, tables, rows_de...]
    dot_general x3 -> x0, matrix products: 9.38 us -> none  [the longest x1 4.03 us: on_device(): preact = jnp.dot(pooled, w_up, preferred_element_type=F32)]
    unnamed x19 -> x11, local copies, waits for them, and re-layouts: 5.12 us -> 5.79 us
where the time goes in v1:
time: 58.9 us; the launch traced here: 58.7 us
  Pallas kernels  51.6 us (88%)
  local copies, waits for them, and re-layouts  5.79 us (10%)
  between operations  1.32 us (2%)
    pallas_call x1, Pallas kernels, on_device(): pl.pallas_call(functools.partial(step_kernel, nz, nx, nh, tables, rows_de...  51.6 us
    unnamed x11, local copies, waits for them, and re-layouts  5.79 us

profile of v1, /device:TPU:0, one launch (start us, length us, event | category | flops | bytes accessed | tf_op | source)
XLA Modules:
  0.0 58.7 jit_solution(8250951373918586818)
XLA Ops:
  1.3 51.6 %step.1 = (f32[32,2048]{1,0:T(8,128)}, f32[2048,128]{1,0:T(8,128)}, f32[16,128]{1,0:T(8,128)}, f32[2,128,128]{2,1,0:T(8,128)}, f32[2,1,128]{2,1,0:T(1,128)}) custom-call(bf16[512,512]{1,0:T(8,128)(2,1)} %pooled.1, bf16[512,2048]{1,0:T(8,128)(2,1)} %w_up.1, bf16[512,2048]{1,0:T(8,128)(2,1)} %grad_out.1, s32[2,8,512]{2,1,0:T(8,128)} %bitcast.15, ...), custom_call_target="tpu_custom_call" | custom-call | tf_op jit(solution)/shard_map/step/pallas_call | solution.py:645
  52.9 0.0 copy-start.1
  52.9 0.0 copy-start
  52.9 0.0 copy-start.2
  52.9 1.7 %copy.24 = f32[32,2048]{1,0:T(8,128)} copy(f32[32,2048]{1,0:T(8,128)} %get-tuple-element.20) | data formatting | bytes 524288
  54.6 2.3 %copy.25 = f32[1,1,2048,128]{3,2,1,0:T(8,128)} copy(f32[1,1,2048,128]{3,2,1,0:T(8,128)} %bitcast.13) | data formatting | bytes 2097152
  56.9 0.0 copy-done.1
  56.9 0.6 %copy.26 = f32[1,1,2048]{2,1,0:T(1,128)} copy(f32[1,1,2048]{2,1,0:T(1,128)S(1)} %bitcast.20) | data formatting | bytes 16384
  57.5 0.0 copy-done
  57.5 0.7 %copy.27 = f32[1,1,2,128,128]{4,3,2,1,0:T(8,128)} copy(f32[1,1,2,128,128]{4,3,2,1,0:T(8,128)S(1)} %bitcast.14) | data formatting | bytes 262144
  58.1 0.0 copy-done.2
  58.1 0.6 copy.28
Async XLA Ops:
  52.9 4.0 %copy-start.1 = (f32[16,128]{1,0:T(8,128)S(1)}, f32[16,128]{1,0:T(8,128)}, u32[]{:S(2)}) copy-start(f32[16,128]{1,0:T(8,128)} %get-tuple-element.12) | copy-start | bytes 24580
  52.9 4.6 %copy-start = (f32[2,128,128]{2,1,0:T(8,128)S(1)}, f32[2,128,128]{2,1,0:T(8,128)}, u32[]{:S(2)}) copy-start(f32[2,128,128]{2,1,0:T(8,128)} %get-tuple-element.13) | copy-start | bytes 393220
  52.9 5.2 %copy-start.2 = (f32[2,1,128]{2,1,0:T(1,128)S(1)}, f32[2,1,128]{2,1,0:T(1,128)}, u32[]{:S(2)}) copy-start(f32[2,1,128]{2,1,0:T(1,128)} %get-tuple-element.14) | copy-start | bytes 3076

commit v2 on v1

v2 whole, which is shorter than its diff:
```python
import functools

import jax
import jax.numpy as jnp
from jax import lax
from jax.experimental import pallas as pl
from jax.experimental.pallas import tpu as pltpu
from jax.sharding import PartitionSpec as P

LEARN_RATE = 0.05
EPSILON = 1e-08
MESH = pl.DeviceIdType.MESH
BLOCKS = 2
SUBS = 2
PIECES = BLOCKS * SUBS
CUTS = 4
UPDATE_TILES = 4
RADIX = 256
ROW_STEP = 2048.0
WEIGHT_STEP = 512.0
F32 = jnp.float32
BF16 = jnp.bfloat16
NT_DIMS = (((1,), (1,)), ((), ()))


def iota(shape, axis):
    return lax.broadcasted_iota(jnp.int32, shape, axis)


def step_kernel(
    nz, nx, nh, tables, rows_dev, tile,
    pooled, w_up, grad_out, owners, rows, lookup_weight, lens, slot_map,
    weight, accum, evict_slots, evict_dest, evict_count,
    grad_up_o, new_weight_o, new_accum_o, held_rows_o, held_accum_o,
    grad_up, new_weight, new_accum, pooled_v, pooled_t, w_v, go_v, delta, own_v, row_v, lw_v, len_v, map_v, weight_v, accum_v,
    es_v, ed_v,
    fown, fsend, ybuf, gat, idx, idxb, grad, rcore, chain, rin, lin, xs, xr, place,
    wide, inv_v, src_v, inv_s, src_s, ev_s, ev_w, ev_a, ev_g, ev_rows, ev_acc, rows_in, acc_in,
    ld_s, sm_s, y_s, y_r, i_s, i_r, azr_s, azl_s, ax_s, ac_s, g_r, gc_r, rc_s, rc_r,
    ch_s, ci_r, xs_s, xr_r, er_s, er_r, ea_s, ea_r, out_s, w_s,
):
    n = nz * nx * 2
    me = lax.axis_index("tbl")
    h = lax.axis_index("hst")
    c = lax.rem(me, 2)
    zx = me // 2
    x = lax.rem(zx, nx)
    z = zx // nx
    other = 1 - c
    batch, hid = grad_out.shape
    feat_n = pooled.shape[1]
    width = ybuf.shape[-1]
    emb = width // tables
    bag = owners.shape[1]
    slots = weight.shape[0]
    list_len = evict_slots.shape[1]
    cap = ev_rows.shape[1]
    out_rows = grad.shape[4]
    cut = hid // CUTS
    piece = batch // PIECES
    block = batch // BLOCKS
    tiles = hid // tile

    def at(zi, xi, ci):
        return (zi * nx + xi) * 2 + ci

    def xof(d):
        return lax.rem(x + d, nx)

    def rcopy(src, dst, s, r, dev):
        return pltpu.make_async_remote_copy(
            src_ref=src, dst_ref=dst, send_sem=s, recv_sem=r,
            device_id=dev, device_id_type=MESH,
        )

    def cols(hh):
        return pl.ds(pl.multiple_of(hh * width, width), width)

    def span(k):
        return pl.ds(k * piece, piece)

    def spanb(k):
        return pl.ds(k * block, block)

    def cutcols(j):
        return pl.ds(j * cut, cut)

    loads = [pltpu.make_async_copy(pooled, pooled_v, ld_s.at[0])]
    w_loads = [
        pltpu.make_async_copy(
            w_up.at[:, pl.ds(j * tile, tile)], w_v.at[:, pl.ds(j * tile, tile)], ld_s.at[1 + j]
        )
        for j in range(tiles)
    ]
    g_loads = [
        pltpu.make_async_copy(grad_out.at[spanb(k)], go_v.at[spanb(k)], ld_s.at[1 + tiles + k])
        for k in range(BLOCKS)
    ]
    base = 1 + tiles + BLOCKS
    small = [
        pltpu.make_async_copy(src, dst, ld_s.at[base + k])
        for k, (src, dst) in enumerate((
            (owners, own_v), (rows, row_v), (lookup_weight, lw_v), (lens, len_v),
            (slot_map, map_v), (evict_slots, es_v), (evict_dest, ed_v),
            (accum, accum_v), (weight, weight_v),
        ))
    ]
    loads[0].start()
    w_loads[0].start()
    g_loads[0].start()
    barrier = pltpu.get_barrier_semaphore()

    def greet(d, carry):
        pl.semaphore_signal(
            barrier, inc=1, device_id={"tbl": lax.rem(me + d, n)}, device_id_type=MESH
        )
        return carry

    lax.fori_loop(1, n, greet, 0)
    for d in range(1, nh):
        pl.semaphore_signal(
            barrier, inc=1, device_id={"hst": lax.rem(h + d, nh)}, device_id_type=MESH
        )
    for copy in w_loads[1:] + g_loads[1:]:
        copy.start()

    def y_copy(d, k):
        h2 = lax.rem(h + d, nh)
        return rcopy(
            fsend.at[d - 1, span(k)], ybuf.at[h, span(k)], y_s, y_r.at[nh - d - 1, k], {"hst": h2}
        )

    def y_arrival(d, k):
        h2 = lax.rem(h + d, nh)
        return rcopy(
            fsend.at[d - 1, span(k)], ybuf.at[h2, span(k)], y_s, y_r.at[d - 1, k],
            {"hst": h2},
        )

    def deltas(k):
        g_loads[k].wait()
        for j in range(tiles):
            if k == 0:
                w_loads[j].wait()
            cs = pl.ds(j * tile, tile)
            p = jnp.dot(pooled_v[spanb(k), :], w_v[:, cs], preferred_element_type=F32)
            s = jax.nn.sigmoid(p)
            g = go_v[spanb(k), cs].astype(F32)
            delta[spanb(k), cs] = (g * s * (1.0 + p * (1.0 - s))).astype(BF16)

    def feats_out(k):
        for d in range(1, nh):
            h2 = lax.rem(h + d, nh)
            part = lax.dot_general(
                delta[spanb(k), :], w_v[cols(h2), :], NT_DIMS, preferred_element_type=F32
            )
            fsend[d - 1, spanb(k)] = part.astype(BF16)
            if k == 0 and d == 1:
                pl.semaphore_wait(barrier, n - 1 + nh - 1)
            for q in range(SUBS):
                y_copy(d, k * SUBS + q).start()

    def feats_own(k):
        fown[spanb(k), :] = lax.dot_general(
            delta[spanb(k), :], w_v[cols(h), :], NT_DIMS, preferred_element_type=F32
        )

    loads[0].wait()
    deltas(0)
    feats_out(0)
    for copy in small:
        copy.start()
    feats_own(0)
    deltas(1)
    feats_out(1)
    feats_own(1)

    def g_copy(slot, k, sem, dev):
        ref = gat.at[slot, span(k)]
        return rcopy(ref, ref, sem, g_r.at[slot // 2, k], {"tbl": dev})


    def right_copy(zi, k):
        return g_copy(at(zi, x, c), k, azr_s, at(z + 1, x, c))

    def left_copy(zi, k):
        return g_copy(at(zi, x, c), k, azl_s, at(z - 1, x, c))

    def x_copy(zi, d, k):
        return g_copy(at(zi, x, c), k, ax_s, at(z, xof(d), c))

    def c_copy(zi, xi, k):
        ref = gat.at[at(zi, xi, c), span(k)]
        return rcopy(ref, ref, ac_s, gc_r.at[zi * nx + xi], {"tbl": at(z, x, other)})

    def arrived(slot, k):
        g_copy(slot, k, ac_s, at(z, x, other)).wait_recv()

    def gather_start(k):
        total = fown[span(k), :]
        for d in range(1, nh):
            y_arrival(d, k).wait_recv()
            total = total + ybuf[lax.rem(h + d, nh), span(k)].astype(F32)
        gat[me, span(k)] = total.astype(BF16)

        @pl.when(z + 1 < nz)
        def _():
            right_copy(z, k).start()

        @pl.when(z >= 1)
        def _():
            left_copy(z, k).start()

        for d in range(1, nx):
            x_copy(z, d, k).start()
        c_copy(z, x, k).start()

    def core_copy(j):
        return rcopy(
            grad.at[j, :, :, other], rcore.at[j], rc_s, rc_r, {"tbl": at(z, x, other)}
        )

    def weight_grad(j):
        part = jnp.dot(pooled_t[...], delta[:, cutcols(j)], preferred_element_type=F32)
        grad[j] = part.reshape(nz, nx, 2, out_rows, cut)
        core_copy(j).start()

    def i_copy(d):
        o = lax.rem(me + d, n)
        return rcopy(idx.at[o], idxb.at[me], i_s, i_r.at[zx], {"tbl": o})

    def i_arrival(first, count):
        ref = idxb.at[pl.ds(first, count)]
        return rcopy(ref, ref, i_s, i_r.at[first // 2], {"tbl": at(z, x, other)})

    gather_start(0)
    for copy in small:
        copy.wait()
    for t in range(tables):
        used = iota((bag, batch), 0) < len_v[t : t + 1, :]
        code = (row_v[t] + 1).astype(F32) * ROW_STEP + lw_v[t].astype(F32) * WEIGHT_STEP
        code = jnp.where(used, code, 0.0)
        for o in range(n):
            idx[o, t : t + 1, :] = jnp.sum(
                jnp.where(own_v[t] == o, code, 0.0), axis=0, keepdims=True
            )
    idxb[me] = idx[me]

    def i_start(d, carry):
        i_copy(d).start()
        return carry

    lax.fori_loop(1, n, i_start, 0)
    pooled_t[...] = pooled_v[...].T

    weight_grad(0)
    for k in range(1, PIECES):
        gather_start(k)
        weight_grad(k)

    place[...] = jnp.zeros_like(place)
    chunk = min(RADIX, rows_dev)

    def proc(*picked):
        codes = [idxb[slot] for slot in picked]
        bags = [gat[slot] for slot in picked]
        for t in range(tables):
            pairs = []
            for code, bag_rows in zip(codes, bags):
                code = code[t : t + 1, :]
                row1 = jnp.floor(code * (1.0 / ROW_STEP))
                wgt = ((code - row1 * ROW_STEP) * (1.0 / WEIGHT_STEP)).astype(BF16)
                pairs.append((row1 - 1.0, wgt, bag_rows[:, t * emb : (t + 1) * emb]))
            ids = iota((chunk, batch), 0).astype(F32).astype(BF16)
            for r0 in range(0, rows_dev, chunk):
                total = None
                for row, wgt, part in pairs:
                    near = row - float(r0)
                    near = jnp.where((near >= 0.0) & (near < float(chunk)), near, -1.0)
                    mark = jnp.where(ids == near.astype(BF16), wgt, jnp.zeros((), BF16))
                    prod = jnp.dot(mark, part, preferred_element_type=F32)
                    total = prod if total is None else total + prod
                place[pl.ds(t * rows_dev + r0, chunk), :] += total

    eye = iota((emb, emb), 0) == iota((emb, emb), 1)
    groups = slots // emb

    inv_copy = pltpu.make_async_copy(inv_v, inv_s, sm_s.at[0])
    src_copy = pltpu.make_async_copy(src_v, src_s, sm_s.at[1])

    def prepare_inverse():
        home = map_v[...].astype(F32)
        high = jnp.floor(home * (1.0 / emb))
        low = home - high * emb
        from_row = iota((1, slots), 1).astype(F32)
        from_high = jnp.floor(from_row * (1.0 / RADIX))
        from_low = from_row - from_high * RADIX
        in_group = iota((groups, slots), 0).astype(F32) == high
        left = jnp.concatenate(
            [jnp.where(in_group, from_high, 0.0), jnp.where(in_group, from_low, 0.0)], axis=0
        ).astype(BF16)
        right = jnp.where(iota((emb, slots), 0).astype(F32) == low, 1.0, 0.0).astype(BF16)
        found = lax.dot_general(left, right, NT_DIMS, preferred_element_type=F32)
        inv = (found[:groups] * RADIX + found[groups:]).astype(jnp.int32)
        inv_v[...] = jnp.clip(inv, 0, slots - 1)
        inv_copy.start()


    def prepare_wide():
        for i in range(groups):
            col = jnp.sum(jnp.where(eye, accum_v[i : i + 1, :], 0.0), axis=1, keepdims=True)
            wide[i * emb : (i + 1) * emb, :] = jnp.broadcast_to(col, (emb, emb))

    def prepare_evict():
        live = iota((1, list_len), 1) < evict_count[0, 0]
        lanes = 8 * -(-nh // 8)
        mine = jnp.where((iota((lanes, list_len), 0) == ed_v[...]) & live, 1.0, 0.0)
        before = jnp.where(iota((list_len, list_len), 0) < iota((list_len, list_len), 1), 1.0, 0.0)
        goal = jnp.dot(mine.astype(BF16), before.astype(BF16), preferred_element_type=F32)
        slot1 = es_v[...].astype(F32) + 1.0
        slot_high = jnp.floor(slot1 * (1.0 / RADIX))
        slot_low = slot1 - slot_high * RADIX
        parts = jnp.where(iota((8, list_len), 0) == 0, slot_high, slot_low).astype(BF16)
        for d in range(nh):
            hot = jnp.where(
                iota((cap, list_len), 0).astype(F32) == goal[d : d + 1], mine[d : d + 1], 0.0
            ).astype(BF16)
            got = lax.dot_general(parts, hot, NT_DIMS, preferred_element_type=F32)
            src = (got[0:1] * RADIX + got[1:2]).astype(jnp.int32)
            src_v[d : d + 1, :] = jnp.clip(src, 0, slots)
        src_copy.start()


    def prepare_fetch(start, stop):
        def slot_of(k, p):
            s1 = src_s[k, p]
            return s1 > 0, jnp.maximum(s1 - 1, 0)

        def ev_fetch(i, carry):
            k = i // (cap // 8)
            p = lax.rem(i, cap // 8) * 8
            for q in range(8):
                ok, s = slot_of(k, p + q)
                ev_w[k, pl.ds(p + q, 1), :] = jnp.where(ok, weight_v[pl.ds(s, 1), :], 0.0)
                ev_a[k, pl.ds(p + q, 1), :] = jnp.where(ok, wide[pl.ds(s, 1), :], 0.0)
                ev_s[k, p + q] = jnp.where(ok, inv_s[s // emb, lax.rem(s, emb)], slots)
            return carry

        lax.fori_loop(start, stop, ev_fetch, 0)

    def rin_copy(t, j):
        return rcopy(
            chain.at[t, j], rin.at[t, j], ch_s, ci_r.at[t, j], {"tbl": at(z + 1, x, c)}
        )

    def lin_copy(t, j):
        return rcopy(
            chain.at[t, j], lin.at[t, j], ch_s, ci_r.at[jnp.where(t == z - 1, nz, t), j],
            {"tbl": at(z - 1, x, c)},
        )

    def lin_arrival(t, j):
        return rcopy(
            chain.at[t, j], lin.at[t, j], ch_s, ci_r.at[jnp.where(t == z, nz, t), j],
            {"tbl": at(z - 1, x, c)},
        )

    def own_sum(t, j, xi):
        return grad[j, t, xi, c] + rcore[j, t, xi]

    def chain_step(t, j, buf, copy):
        for xi in range(nx):
            s = own_sum(t, j, xi)
            if buf is not None:
                s = s + buf[t, j, xi].astype(F32)
            chain[t, j, xi] = s.astype(BF16)
        copy(t, j).start()


    def chain_heads():
        rcopy(rcore, rcore, rc_s, rc_r, {"tbl": at(z, x, other)}).wait_recv()

        @pl.when(z == 0)
        def _():
            def body(i, carry):
                for j in range(CUTS):
                    chain_step(nz - 1 - i, j, None, rin_copy)
                return carry

            lax.fori_loop(0, nz - 1, body, 0)

        @pl.when(z == nz - 1)
        def _():
            def body(i, carry):
                for j in range(CUTS):
                    chain_step(i, j, None, lin_copy)
                return carry

            lax.fori_loop(0, nz - 1, body, 0)

    def xs_copy(d, j):
        x2 = xof(d)
        return rcopy(xs.at[d - 1, j], xr.at[x, j], xs_s, xr_r.at[nx - d - 1], {"tbl": at(z, x2, c)})

    def xs_arrival(d):
        x2 = xof(d)
        return rcopy(xs.at[d - 1], xr.at[x2], xs_s, xr_r.at[d - 1], {"tbl": at(z, x2, c)})

    def finish_cut(j):
        @pl.when(z >= 1)
        def _():
            rin_copy(z, j).wait_recv()
            for xi in range(nx):
                grad[j, z, xi, c] += rin[z, j, xi].astype(F32)

        @pl.when(z + 1 < nz)
        def _():
            lin_arrival(z, j).wait_recv()
            for xi in range(nx):
                grad[j, z, xi, c] += lin[z, j, xi].astype(F32)

        for d in range(1, nx):
            xs[d - 1, j] = own_sum(z, j, xof(d)).astype(BF16)
            xs_copy(d, j).start()

    def from_z(zi, k, open_end, onward):
        arrived(at(zi, x, c), k)

        @pl.when(open_end)
        def _():
            onward(zi, k).start()

        for dx in range(1, nx):
            x_copy(zi, dx, k).start()
        c_copy(zi, x, k).start()

    both = jnp.minimum(z, nz - 1 - z)

    def ring(e):
        dist = (e + 1) // 2
        near = jnp.where(lax.rem(e, 2) == 1, z - dist, z + dist)
        dist = e - both
        far = jnp.where(z - dist >= 0, z - dist, z + dist)
        return jnp.where(e <= 2 * both, near, far)

    def from_x(i):
        head = i < PIECES
        i2 = i - PIECES
        paired = i2 < 2 * PIECES * both
        r = lax.rem(i2, 2 * PIECES)
        i3 = i2 - 2 * PIECES * both
        e = jnp.where(
            head, 0,
            jnp.where(
                paired, 1 + 2 * (i2 // (2 * PIECES)) + lax.rem(r, 2), 1 + 2 * both + i3 // PIECES
            ),
        )
        k = jnp.where(head, i, jnp.where(paired, r // 2, lax.rem(i3, PIECES)))
        zi = ring(e)
        for dx in range(1, nx):
            arrived(at(zi, xof(dx), c), k)
            c_copy(zi, xof(dx), k).start()

    def expect(zi, xi):
        mine = at(zi, xi, c)

        @pl.when(mine != me)
        def _():
            i_arrival(at(zi, xi, 0), 2).wait_recv()

        @pl.when(mine == me)
        def _():
            i_arrival(at(zi, xi, 0), 1).wait_recv()

        return mine

    def core_slot(zi, xi):
        slot = at(zi, xi, other)
        ref = gat.at[slot]
        rcopy(ref, ref, ac_s, gc_r.at[zi * nx + xi], {"tbl": at(z, x, other)}).wait_recv()
        return slot

    def pair_proc(zi, xi):
        mine = expect(zi, xi)
        proc(mine, core_slot(zi, xi))

    zr = nz - 1 - z

    def step_body(i, carry):
        j = i // PIECES + 1
        k = lax.rem(i, PIECES)
        s = j - 1

        @pl.when(z - j >= 0)
        def _():
            from_z(z - j, k, z + 1 < nz, right_copy)

        @pl.when(z + j < nz)
        def _():
            from_z(z + j, k, z >= 1, left_copy)

        from_x(i)

        @pl.when((s <= nz - 2) & (z >= 1) & (z <= s))
        def _():
            t = nz - 1 - s + z
            rin_copy(t, k).wait_recv()
            chain_step(t, k, rin, rin_copy)

        @pl.when((s <= nz - 2) & (zr >= 1) & (zr <= s))
        def _():
            t = s - zr
            lin_arrival(t, k).wait_recv()
            chain_step(t, k, lin, lin_copy)

        @pl.when(s == nz - 1)
        def _():
            finish_cut(k)

        @pl.when(i == 1)
        def _():
            chain_heads()
            prepare_inverse()

        @pl.when(i == 2)
        def _():
            prepare_wide()

        @pl.when(i == 3)
        def _():
            prepare_evict()

        @pl.when(i == 2 * PIECES - 1)
        def _():
            inv_copy.wait()
            src_copy.wait()
            prepare_fetch(0, nh * cap // 16)

        @pl.when(i == 3 * PIECES - 1)
        def _():
            prepare_fetch(nh * cap // 16, nh * cap // 8)

        side = lax.rem(k, 2) == 0
        near = k < 2
        zi = jnp.where(near, jnp.where(side, z - s, z + s), ring(jnp.maximum(s - 1, 0)))
        on_line = near & ((s >= 1) | side) & (zi >= 0) & (zi < nz)
        on_side = (k == 2) & (s >= 1)

        @pl.when(on_line | on_side)
        def _():
            def one(dx, carry):
                pair_proc(zi, xof(dx))
                return carry

            lax.fori_loop(jnp.where(near, 0, 1), jnp.where(near, 1, nx), one, 0)

        return carry

    lax.fori_loop(0, PIECES * nz, step_body, 0)
    for dx in range(1, nx):
        proc(expect(ring(nz - 1), xof(dx)))
        proc(core_slot(ring(nz - 1), xof(dx)))

    def gathered(first):
        picks = []
        for q in range(8):
            picks.append(place[pl.ds(first(q), 1), :])
        return jnp.concatenate(picks, axis=0)

    def ev_gather(i, carry):
        k = i // (cap // 8)
        p = lax.rem(i, cap // 8) * 8
        ev_g[k, pl.ds(pl.multiple_of(p, 8), 8), :] = gathered(lambda q: ev_s[k, p + q])
        return carry

    lax.fori_loop(0, nh * cap // 8, ev_gather, 0)

    def er_copy(d, slot):
        k = lax.rem(h + d, nh)
        return rcopy(ev_rows.at[k], rows_in.at[slot], er_s, er_r.at[slot], {"hst": k})

    def ea_copy(d, slot):
        k = lax.rem(h + d, nh)
        return rcopy(ev_acc.at[k], acc_in.at[slot], ea_s, ea_r.at[slot], {"hst": k})

    for d in range(1, nh + 1):
        k = lax.rem(h + d, nh)
        for r0 in range(0, cap, emb):
            span_k = pl.ds(r0, emb)
            g = ev_g[k, span_k]
            acc = ev_a[k, span_k] + jnp.mean(g * g, axis=1, keepdims=True)
            ev_rows[k, span_k] = ev_w[k, span_k] - LEARN_RATE * g / (jnp.sqrt(acc) + EPSILON)
            ev_acc[k, :, span_k] = jnp.sum(jnp.where(eye, acc, 0.0), axis=0, keepdims=True)
        if d < nh:
            er_copy(d, h).start()
            ea_copy(d, h).start()
    def held_out(buf, acc, k):
        return (
            pltpu.make_async_copy(buf.at[k], held_rows_o.at[k], out_s.at[2 + k]),
            pltpu.make_async_copy(acc.at[k], held_accum_o.at[k], out_s.at[2 + nh + k]),
        )

    for copy in held_out(ev_rows, ev_acc, h):
        copy.start()

    batch_tiles = max(u for u in (1, 2, UPDATE_TILES) if groups % u == 0)
    spread = batch_tiles * emb

    def weight_out(i):
        at_i = pl.ds(pl.multiple_of(i * spread, spread), spread)
        return pltpu.make_async_copy(new_weight.at[at_i], new_weight_o.at[at_i], w_s)

    def update(i2, carry):
        for u in range(batch_tiles):
            i = i2 * batch_tiles + u
            total = jnp.zeros((8, emb), F32)
            for b in range(emb // 8):
                rows_b = pl.ds(pl.multiple_of(i * emb + b * 8, 8), 8)
                g = gathered(lambda q: inv_s[i, b * 8 + q])
                acc = wide[rows_b, :] + jnp.mean(g * g, axis=1, keepdims=True)
                new_weight[rows_b, :] = weight_v[rows_b, :] - LEARN_RATE * g / (
                    jnp.sqrt(acc) + EPSILON
                )
                diag = iota((8, emb), 1) == iota((8, emb), 0) + b * 8
                total = total + jnp.where(diag, acc, 0.0)
            new_accum[pl.ds(i, 1), :] = jnp.sum(total, axis=0, keepdims=True)
        weight_out(i2).start()
        return carry

    lax.fori_loop(0, groups // batch_tiles, update, 0)
    accum_out = pltpu.make_async_copy(new_accum, new_accum_o, out_s.at[0])
    accum_out.start()

    for d in range(1, nx):
        xs_arrival(d).wait_recv()
    for j in range(CUTS):
        s = own_sum(z, j, x)
        for d in range(1, nx):
            s = s + xr[xof(d), j].astype(F32)
        grad_up[:, cutcols(j)] = s
    grad_out_copy = pltpu.make_async_copy(grad_up, grad_up_o, out_s.at[1])
    grad_out_copy.start()

    for d in range(1, nh):
        k = lax.rem(h + d, nh)
        er_copy(d, k).wait_recv()
        ea_copy(d, k).wait_recv()
        for copy in held_out(rows_in, acc_in, k):
            copy.start()

    def all_sent(ref, sem, recv, dev):
        rcopy(ref, ref, sem, recv, dev).wait_send()

    core_dev = {"tbl": at(z, x, other)}
    if nh > 1:
        host_dev = {"hst": lax.rem(h + 1, nh)}
        all_sent(ev_rows.at[pl.ds(0, nh - 1)], er_s, er_r.at[0], host_dev)
        all_sent(ev_acc.at[pl.ds(0, nh - 1)], ea_s, ea_r.at[0], host_dev)
        all_sent(fsend, y_s, y_r.at[0, 0], host_dev)
    all_sent(rcore, rc_s, rc_r, core_dev)
    all_sent(idx.at[pl.ds(0, n - 1)], i_s, i_r.at[0], core_dev)
    all_sent(gat.at[pl.ds(0, nz * nx)], ac_s, gc_r.at[0], core_dev)
    if nx > 1:
        all_sent(xs, xs_s, xr_r.at[0], core_dev)
        all_sent(gat.at[pl.ds(0, nz * (nx - 1))], ax_s, gc_r.at[0], core_dev)
    if nz > 1:
        all_sent(chain.at[pl.ds(0, nz - 1)], ch_s, ci_r.at[0, 0], core_dev)
    for q in range(nz - 1):

        @pl.when(z == q)
        def _(q=q):
            all_sent(gat.at[pl.ds(0, q + 1)], azr_s, gc_r.at[0], core_dev)

        @pl.when(zr == q)
        def _(q=q):
            all_sent(gat.at[pl.ds(0, q + 1)], azl_s, gc_r.at[0], core_dev)

    pltpu.make_async_copy(new_weight, new_weight_o, w_s).wait()
    accum_out.wait()
    grad_out_copy.wait()
    for d in range(nh):
        k = lax.rem(h + d, nh)
        buf, acc = (ev_rows, ev_acc) if d == 0 else (rows_in, acc_in)
        for copy in held_out(buf, acc, k):
            copy.wait()


def write_kernel(*refs):
    sems = refs[10]
    copies = [pltpu.make_async_copy(refs[k], refs[5 + k], sems.at[k]) for k in range(5)]
    for copy in copies:
        copy.start()
    for copy in copies:
        copy.wait()


def on_device(
    nz, nx,
    pooled, w_up, grad_out, owners, rows, lookup_weight, lens, slot_map,
    cache_weight, cache_accum, evict_slots, evict_dest, evict_count,
):
    tables, batch, bag = owners.shape
    slots = slot_map.shape[-1]
    rows_dev = slots // tables
    emb = cache_weight.shape[-1]
    n = lax.axis_size("tbl")
    nh = lax.axis_size("hst")
    feat_n, hid = w_up.shape
    out_rows = feat_n // n
    width = tables * emb
    groups = slots // emb
    list_len = evict_slots.shape[-1]
    cap = list_len // 2
    cut = hid // CUTS
    tile = min(512, hid)

    dma = pltpu.SemaphoreType.DMA
    anyspace = pl.BlockSpec(memory_space=pltpu.HBM)
    i32 = jnp.int32
    grad_up, new_weight, new_accum, held_rows, held_accum = pl.pallas_call(
        functools.partial(step_kernel, nz, nx, nh, tables, rows_dev, tile),
        out_shape=(
            jax.ShapeDtypeStruct((out_rows, hid), F32),
            jax.ShapeDtypeStruct((slots, emb), F32),
            jax.ShapeDtypeStruct((groups, emb), F32),
            jax.ShapeDtypeStruct((nh, cap, emb), F32),
            jax.ShapeDtypeStruct((nh, 1, cap), F32),
        ),
        in_specs=[anyspace] * 12 + [pl.BlockSpec(memory_space=pltpu.SMEM)],
        out_specs=(pl.BlockSpec(memory_space=pl.ANY),) * 5,
        scratch_shapes=[
            pltpu.VMEM((out_rows, hid), F32),
            pltpu.VMEM((slots, emb), F32),
            pltpu.VMEM((groups, emb), F32),
            pltpu.VMEM((batch, feat_n), BF16),
            pltpu.VMEM((feat_n, batch), BF16),
            pltpu.VMEM((feat_n, hid), BF16),
            pltpu.VMEM((batch, hid), BF16),
            pltpu.VMEM((batch, hid), BF16),
            pltpu.VMEM((tables, bag, batch), i32),
            pltpu.VMEM((tables, bag, batch), i32),
            pltpu.VMEM((tables, bag, batch), BF16),
            pltpu.VMEM((tables, batch), i32),
            pltpu.VMEM((1, slots), i32),
            pltpu.VMEM((slots, emb), F32),
            pltpu.VMEM((groups, emb), F32),
            pltpu.VMEM((1, list_len), i32),
            pltpu.VMEM((1, list_len), i32),
            pltpu.VMEM((batch, width), F32),
            pltpu.VMEM((nh - 1, batch, width), BF16),
            pltpu.VMEM((nh, batch, width), BF16),
            pltpu.VMEM((n, batch, width), BF16),
            pltpu.VMEM((n, tables, batch), F32),
            pltpu.VMEM((n, tables, batch), F32),
            pltpu.VMEM((CUTS, nz, nx, 2, out_rows, cut), F32),
            pltpu.VMEM((CUTS, nz, nx, out_rows, cut), F32),
            pltpu.VMEM((nz, CUTS, nx, out_rows, cut), BF16),
            pltpu.VMEM((nz, CUTS, nx, out_rows, cut), BF16),
            pltpu.VMEM((nz, CUTS, nx, out_rows, cut), BF16),
            pltpu.VMEM((max(nx - 1, 1), CUTS, out_rows, cut), BF16),
            pltpu.VMEM((nx, CUTS, out_rows, cut), BF16),
            pltpu.VMEM((slots + 8, emb), F32),
            pltpu.VMEM((slots, emb), F32),
            pltpu.VMEM((groups, emb), i32),
            pltpu.VMEM((nh, cap), i32),
            pltpu.SMEM((groups, emb), i32),
            pltpu.SMEM((nh, cap), i32),
            pltpu.SMEM((nh, cap), i32),
            pltpu.VMEM((nh, cap, emb), F32),
            pltpu.VMEM((nh, cap, emb), F32),
            pltpu.VMEM((nh, cap, emb), F32),
            pltpu.VMEM((nh, cap, emb), F32),
            pltpu.VMEM((nh, 1, cap), F32),
            pltpu.VMEM((nh, cap, emb), F32),
            pltpu.VMEM((nh, 1, cap), F32),
            dma((1 + hid // tile + BLOCKS + 9,)), dma((2,)),
            dma, dma((max(nh - 1, 1), PIECES)), dma, dma((nz * nx,)),
            dma, dma, dma, dma, dma((nz * nx, PIECES)), dma((nz * nx,)), dma, dma,
            dma, dma((nz + 1, CUTS)), dma, dma((max(nx - 1, 1),)),
            dma, dma((nh,)), dma, dma((nh,)), dma((2 + 2 * nh,)), dma,
        ],
        compiler_params=pltpu.CompilerParams(
            collective_id=0, has_side_effects=True, vmem_limit_bytes=48 * 1024 * 1024
        ),
        name="step",
    )(*[pltpu.with_memory_space_constraint(v, pltpu.HBM) for v in (
        pooled, w_up, grad_out,
        jnp.transpose(owners, (0, 2, 1)), jnp.transpose(rows, (0, 2, 1)),
        jnp.transpose(lookup_weight, (0, 2, 1)), lens, slot_map.reshape(1, slots),
        cache_weight.reshape(slots, emb), cache_accum.reshape(groups, emb),
        evict_slots.reshape(1, list_len), evict_dest.reshape(1, list_len),
    )], evict_count)
    outs = (grad_up, new_weight, new_accum, held_rows, held_accum)
    hbm = pl.BlockSpec(memory_space=pltpu.HBM)
    grad_up, new_weight, new_accum, held_rows, held_accum = pl.pallas_call(
        write_kernel,
        out_shape=tuple(jax.ShapeDtypeStruct(v.shape, v.dtype) for v in outs),
        in_specs=[pl.BlockSpec(memory_space=pl.ANY)] * 5,
        out_specs=(hbm,) * 5,
        scratch_shapes=[dma((5,))],
        compiler_params=pltpu.CompilerParams(vmem_limit_bytes=1024 * 1024),
        name="write",
    )(*outs)
    return (
        grad_up,
        new_weight[None, None],
        new_accum.reshape(1, 1, slots),
        held_rows[None, None],
        held_accum.reshape(1, 1, nh, cap),
    )


def solution(mesh):
    n, nh = mesh.shape["tbl"], mesh.shape["hst"]
    nx = nh if n % (2 * nh) == 0 else 1
    nz = n // (2 * nx)
    placed = (
        P("tbl", None),
        P(None, "hst"),
        P("tbl", "hst"),
        P("hst", "tbl", None),
        P("hst", "tbl", None),
        P("hst", "tbl", None),
        P("hst", "tbl"),
        P("tbl", "hst", None),
        P("tbl", "hst", None, None),
        P("tbl", "hst", None),
        P("tbl", "hst", None),
        P("tbl", "hst", None),
        P("tbl", "hst"),
    )
    return jax.shard_map(
        functools.partial(on_device, nz, nx),
        mesh=mesh,
        in_specs=placed,
        out_specs=(
            P("tbl", "hst"),
            P("tbl", "hst", None, None),
            P("tbl", "hst", None),
            P("tbl", "hst", None, None, None),
            P("tbl", "hst", None, None),
        ),
        check_vma=False,
    )
```

time: 58.9 us -> 45.5 us (0.77)
  Pallas kernels: 51.6 us -> 44.1 us
  local copies, waits for them, and re-layouts: 5.79 us -> 0 us
    pallas_call x1, Pallas kernels: 51.6 us -> 42.9 us  [on_device(): pl.pallas_call(functools.partial(step_kernel, nz, nx, nh, tables, rows_de...]
    unnamed x11 -> x0, local copies, waits for them, and re-layouts: 5.79 us -> none
    pallas_call x0 -> x1, Pallas kernels: none -> 1.14 us  [on_device(): pl.pallas_call(write_kernel, out_shape=tuple((jax.ShapeDtypeStruct(v.shap...]
where the time goes in v2:
time: 45.5 us; the launch traced here: 45.4 us
  Pallas kernels  44.1 us (97%)
  between operations  1.29 us (3%)
    pallas_call x1, Pallas kernels, on_device(): pl.pallas_call(functools.partial(step_kernel, nz, nx, nh, tables, rows_de...  42.9 us
    pallas_call x1, Pallas kernels, on_device(): pl.pallas_call(write_kernel, out_shape=tuple((jax.ShapeDtypeStruct(v.shap...  1.14 us

profile of v2, /device:TPU:0, one launch (start us, length us, event | category | flops | bytes accessed | tf_op | source)
XLA Modules:
  0.0 45.4 jit_solution(4632184060434564413)
XLA Ops:
  1.3 42.9 %step.1 = (f32[32,2048]{1,0:T(8,128)S(1)}, f32[2048,128]{1,0:T(8,128)S(1)}, f32[16,128]{1,0:T(8,128)S(1)}, f32[2,128,128]{2,1,0:T(8,128)S(1)}, f32[2,1,128]{2,1,0:T(1,128)S(1)}) custom-call(bf16[512,512]{1,0:T(8,128)(2,1)} %pooled.1, bf16[512,2048]{1,0:T(8,128)(2,1)} %w_up.1, bf16[512,2048]{1,0:T(8,128)(2,1)} %grad_out.1, s32[2,8,512]{2,1,0:T(8,128)} %bitcast.13, ...), custom_call_target="tpu_custom_call" | custom-call | tf_op jit(solution)/shard_map/step/pallas_call | solution.py:720
  44.2 1.1 %write.1 = (f32[32,2048]{1,0:T(8,128)}, f32[2048,128]{1,0:T(8,128)}, f32[16,128]{1,0:T(8,128)}, f32[2,128,128]{2,1,0:T(8,128)}, f32[2,1,128]{2,1,0:T(1,128)}) custom-call(f32[32,2048]{1,0:T(8,128)S(1)} %get-tuple-element.15.refs_0_, f32[2048,128]{1,0:T(8,128)S(1)} %get-tuple-element.16.refs_1_, f32[16,128]{1,0:T(8,128)S(1)} %get-tuple-element.17.refs_2_, ...), custom_call_target="tpu_custom_call" | custom-call | tf_op jit(solution)/shard_map/write/pallas_call | solution.py:795

commit v3 on v2

--- a/solution.py
+++ b/solution.py
@@ -35,7 +35,7 @@
     grad_up, new_weight, new_accum, pooled_v, pooled_t, w_v, go_v, delta, own_v, row_v, lw_v, len_v, map_v, weight_v, accum_v,
     es_v, ed_v,
     fown, fsend, ybuf, gat, idx, idxb, grad, rcore, chain, rin, lin, xs, xr, place,
-    wide, inv_v, src_v, inv_s, src_s, ev_s, ev_w, ev_a, ev_g, ev_rows, ev_acc, rows_in, acc_in,
+    wide, inv_v, src_v, inv_s, src_s, ev_s, ev_w, ev_a, ev_g, ev_rows, ev_acc, rows_in, acc_in, ev_half, half_in,
     ld_s, sm_s, y_s, y_r, i_s, i_r, azr_s, azl_s, ax_s, ac_s, g_r, gc_r, rc_s, rc_r,
     ch_s, ci_r, xs_s, xr_r, er_s, er_r, ea_s, ea_r, out_s, w_s,
 ):
@@ -121,7 +121,7 @@
         pl.semaphore_signal(
             barrier, inc=1, device_id={"hst": lax.rem(h + d, nh)}, device_id_type=MESH
         )
-    for copy in w_loads[1:] + g_loads[1:]:
+    for copy in w_loads[1:] + small + g_loads[1:]:
         copy.start()
 
     def y_copy(d, k):
@@ -157,7 +157,11 @@
             fsend[d - 1, spanb(k)] = part.astype(BF16)
             if k == 0 and d == 1:
                 pl.semaphore_wait(barrier, n - 1 + nh - 1)
-            for q in range(SUBS):
+            y_copy(d, k * SUBS).start()
+
+    def feats_rest(k):
+        for q in range(1, SUBS):
+            for d in range(1, nh):
                 y_copy(d, k * SUBS + q).start()
 
     def feats_own(k):
@@ -165,75 +169,17 @@
             delta[spanb(k), :], w_v[cols(h), :], NT_DIMS, preferred_element_type=F32
         )
 
+    def i_copy(d):
+        o = lax.rem(me + d, n)
+        return rcopy(idx.at[o], idxb.at[me], i_s, i_r.at[zx], {"tbl": o})
+
+    def i_arrival(first, count):
+        ref = idxb.at[pl.ds(first, count)]
+        return rcopy(ref, ref, i_s, i_r.at[first // 2], {"tbl": at(z, x, other)})
+
     loads[0].wait()
     deltas(0)
     feats_out(0)
-    for copy in small:
-        copy.start()
-    feats_own(0)
-    deltas(1)
-    feats_out(1)
-    feats_own(1)
-
-    def g_copy(slot, k, sem, dev):
-        ref = gat.at[slot, span(k)]
-        return rcopy(ref, ref, sem, g_r.at[slot // 2, k], {"tbl": dev})
-
-
-    def right_copy(zi, k):
-        return g_copy(at(zi, x, c), k, azr_s, at(z + 1, x, c))
-
-    def left_copy(zi, k):
-        return g_copy(at(zi, x, c), k, azl_s, at(z - 1, x, c))
-
-    def x_copy(zi, d, k):
-        return g_copy(at(zi, x, c), k, ax_s, at(z, xof(d), c))
-
-    def c_copy(zi, xi, k):
-        ref = gat.at[at(zi, xi, c), span(k)]
-        return rcopy(ref, ref, ac_s, gc_r.at[zi * nx + xi], {"tbl": at(z, x, other)})
-
-    def arrived(slot, k):
-        g_copy(slot, k, ac_s, at(z, x, other)).wait_recv()
-
-    def gather_start(k):
-        total = fown[span(k), :]
-        for d in range(1, nh):
-            y_arrival(d, k).wait_recv()
-            total = total + ybuf[lax.rem(h + d, nh), span(k)].astype(F32)
-        gat[me, span(k)] = total.astype(BF16)
-
-        @pl.when(z + 1 < nz)
-        def _():
-            right_copy(z, k).start()
-
-        @pl.when(z >= 1)
-        def _():
-            left_copy(z, k).start()
-
-        for d in range(1, nx):
-            x_copy(z, d, k).start()
-        c_copy(z, x, k).start()
-
-    def core_copy(j):
-        return rcopy(
-            grad.at[j, :, :, other], rcore.at[j], rc_s, rc_r, {"tbl": at(z, x, other)}
-        )
-
-    def weight_grad(j):
-        part = jnp.dot(pooled_t[...], delta[:, cutcols(j)], preferred_element_type=F32)
-        grad[j] = part.reshape(nz, nx, 2, out_rows, cut)
-        core_copy(j).start()
-
-    def i_copy(d):
-        o = lax.rem(me + d, n)
-        return rcopy(idx.at[o], idxb.at[me], i_s, i_r.at[zx], {"tbl": o})
-
-    def i_arrival(first, count):
-        ref = idxb.at[pl.ds(first, count)]
-        return rcopy(ref, ref, i_s, i_r.at[first // 2], {"tbl": at(z, x, other)})
-
-    gather_start(0)
     for copy in small:
         copy.wait()
     for t in range(tables):
@@ -251,8 +197,66 @@
         return carry
 
     lax.fori_loop(1, n, i_start, 0)
+
+    feats_rest(0)
+    feats_own(0)
+    deltas(1)
+    feats_out(1)
+    feats_own(1)
+    feats_rest(1)
+
+    def g_copy(slot, k, sem, dev):
+        ref = gat.at[slot, span(k)]
+        return rcopy(ref, ref, sem, g_r.at[slot // 2, k], {"tbl": dev})
+
+
+    def right_copy(zi, k):
+        return g_copy(at(zi, x, c), k, azr_s, at(z + 1, x, c))
+
+    def left_copy(zi, k):
+        return g_copy(at(zi, x, c), k, azl_s, at(z - 1, x, c))
+
+    def x_copy(zi, d, k):
+        return g_copy(at(zi, x, c), k, ax_s, at(z, xof(d), c))
+
+    def c_copy(zi, xi, k):
+        ref = gat.at[at(zi, xi, c), span(k)]
+        return rcopy(ref, ref, ac_s, gc_r.at[zi * nx + xi], {"tbl": at(z, x, other)})
+
+    def arrived(slot, k):
+        g_copy(slot, k, ac_s, at(z, x, other)).wait_recv()
+
+    def gather_start(k):
+        total = fown[span(k), :]
+        for d in range(1, nh):
+            y_arrival(d, k).wait_recv()
+            total = total + ybuf[lax.rem(h + d, nh), span(k)].astype(F32)
+        gat[me, span(k)] = total.astype(BF16)
+
+        @pl.when(z + 1 < nz)
+        def _():
+            right_copy(z, k).start()
+
+        @pl.when(z >= 1)
+        def _():
+            left_copy(z, k).start()
+
+        for d in range(1, nx):
+            x_copy(z, d, k).start()
+        c_copy(z, x, k).start()
+
+    def core_copy(j):
+        return rcopy(
+            grad.at[j, :, :, other], rcore.at[j], rc_s, rc_r, {"tbl": at(z, x, other)}
+        )
+
+    def weight_grad(j):
+        part = jnp.dot(pooled_t[...], delta[:, cutcols(j)], preferred_element_type=F32)
+        grad[j] = part.reshape(nz, nx, 2, out_rows, cut)
+        core_copy(j).start()
+
+    gather_start(0)
     pooled_t[...] = pooled_v[...].T
-
     weight_grad(0)
     for k in range(1, PIECES):
         gather_start(k)
@@ -542,9 +546,13 @@
 
         side = lax.rem(k, 2) == 0
         near = k < 2
-        zi = jnp.where(near, jnp.where(side, z - s, z + s), ring(jnp.maximum(s - 1, 0)))
-        on_line = near & ((s >= 1) | side) & (zi >= 0) & (zi < nz)
-        on_side = (k == 2) & (s >= 1)
+        end = s == nz - 1
+        below = z - s
+        line = jnp.where(side & ((below >= 0) | ~end), below, z + s)
+        near = near & (side | ((s >= 1) & ~end))
+        zi = jnp.where(near, line, ring(jnp.maximum(s - 1, 0)))
+        on_line = near & (zi >= 0) & (zi < nz)
+        on_side = (k == jnp.where(end, 1, 2)) & (s >= 1)
 
         @pl.when(on_line | on_side)
         def _():
@@ -567,17 +575,22 @@
             picks.append(place[pl.ds(first(q), 1), :])
         return jnp.concatenate(picks, axis=0)
 
+    step = 64
+
     def ev_gather(i, carry):
-        k = i // (cap // 8)
-        p = lax.rem(i, cap // 8) * 8
-        ev_g[k, pl.ds(pl.multiple_of(p, 8), 8), :] = gathered(lambda q: ev_s[k, p + q])
+        k = i // (cap // step)
+        p = lax.rem(i, cap // step) * step
+        for b in range(0, step, 8):
+            ev_g[k, pl.ds(pl.multiple_of(p + b, 8), 8), :] = gathered(
+                lambda q: ev_s[k, p + b + q]
+            )
         return carry
 
-    lax.fori_loop(0, nh * cap // 8, ev_gather, 0)
+    lax.fori_loop(0, nh * cap // step, ev_gather, 0)
 
     def er_copy(d, slot):
         k = lax.rem(h + d, nh)
-        return rcopy(ev_rows.at[k], rows_in.at[slot], er_s, er_r.at[slot], {"hst": k})
+        return rcopy(ev_half.at[k], half_in.at[slot], er_s, er_r.at[slot], {"hst": k})
 
     def ea_copy(d, slot):
         k = lax.rem(h + d, nh)
@@ -592,6 +605,7 @@
             ev_rows[k, span_k] = ev_w[k, span_k] - LEARN_RATE * g / (jnp.sqrt(acc) + EPSILON)
             ev_acc[k, :, span_k] = jnp.sum(jnp.where(eye, acc, 0.0), axis=0, keepdims=True)
         if d < nh:
+            ev_half[k] = ev_rows[k].astype(BF16)
             er_copy(d, h).start()
             ea_copy(d, h).start()
     def held_out(buf, acc, k):
@@ -645,6 +659,7 @@
         k = lax.rem(h + d, nh)
         er_copy(d, k).wait_recv()
         ea_copy(d, k).wait_recv()
+        rows_in[k] = half_in[k].astype(F32)
         for copy in held_out(rows_in, acc_in, k):
             copy.start()
 
@@ -654,7 +669,7 @@
     core_dev = {"tbl": at(z, x, other)}
     if nh > 1:
         host_dev = {"hst": lax.rem(h + 1, nh)}
-        all_sent(ev_rows.at[pl.ds(0, nh - 1)], er_s, er_r.at[0], host_dev)
+        all_sent(ev_half.at[pl.ds(0, nh - 1)], er_s, er_r.at[0], host_dev)
         all_sent(ev_acc.at[pl.ds(0, nh - 1)], ea_s, ea_r.at[0], host_dev)
         all_sent(fsend, y_s, y_r.at[0, 0], host_dev)
     all_sent(rcore, rc_s, rc_r, core_dev)
@@ -773,6 +788,8 @@
             pltpu.VMEM((nh, 1, cap), F32),
             pltpu.VMEM((nh, cap, emb), F32),
             pltpu.VMEM((nh, 1, cap), F32),
+            pltpu.VMEM((nh, cap, emb), BF16),
+            pltpu.VMEM((nh, cap, emb), BF16),
             dma((1 + hid // tile + BLOCKS + 9,)), dma((2,)),
             dma, dma((max(nh - 1, 1), PIECES)), dma, dma((nz * nx,)),
             dma, dma, dma, dma, dma((nz * nx, PIECES)), dma((nz * nx,)), dma, dma,

time: 45.5 us -> 43.7 us (0.960)
  Pallas kernels: 44.1 us -> 42.3 us
    pallas_call x1, Pallas kernels: 42.9 us -> 41.1 us  [on_device(): pl.pallas_call(functools.partial(step_kernel, nz, nx, nh, tables, rows_de...]
where the time goes in v3:
time: 43.7 us; the launch traced here: 43.6 us
  Pallas kernels  42.3 us (97%)
  between operations  1.29 us (3%)
    pallas_call x1, Pallas kernels, on_device(): pl.pallas_call(functools.partial(step_kernel, nz, nx, nh, tables, rows_de...  41.1 us
    pallas_call x1, Pallas kernels, on_device(): pl.pallas_call(write_kernel, out_shape=tuple((jax.ShapeDtypeStruct(v.shap...  1.14 us

profile of v3, /device:TPU:0, one launch (start us, length us, event | category | flops | bytes accessed | tf_op | source)
XLA Modules:
  0.0 43.6 jit_solution(2891327518093381389)
XLA Ops:
  1.3 41.1 %step.1 = (f32[32,2048]{1,0:T(8,128)S(1)}, f32[2048,128]{1,0:T(8,128)S(1)}, f32[16,128]{1,0:T(8,128)S(1)}, f32[2,128,128]{2,1,0:T(8,128)S(1)}, f32[2,1,128]{2,1,0:T(1,128)S(1)}) custom-call(bf16[512,512]{1,0:T(8,128)(2,1)} %pooled.1, bf16[512,2048]{1,0:T(8,128)(2,1)} %w_up.1, bf16[512,2048]{1,0:T(8,128)(2,1)} %grad_out.1, s32[2,8,512]{2,1,0:T(8,128)} %bitcast.13, ...), custom_call_target="tpu_custom_call" | custom-call | tf_op jit(solution)/shard_map/step/pallas_call | solution.py:735
  42.4 1.1 %write.1 = (f32[32,2048]{1,0:T(8,128)}, f32[2048,128]{1,0:T(8,128)}, f32[16,128]{1,0:T(8,128)}, f32[2,128,128]{2,1,0:T(8,128)}, f32[2,1,128]{2,1,0:T(1,128)}) custom-call(f32[32,2048]{1,0:T(8,128)S(1)} %get-tuple-element.15.refs_0_, f32[2048,128]{1,0:T(8,128)S(1)} %get-tuple-element.16.refs_1_, f32[16,128]{1,0:T(8,128)S(1)} %get-tuple-element.17.refs_2_, ...), custom_call_target="tpu_custom_call" | custom-call | tf_op jit(solution)/shard_map/write/pallas_call | solution.py:812

commit v4 on v2

--- a/solution.py
+++ b/solution.py
@@ -35,7 +35,7 @@
     grad_up, new_weight, new_accum, pooled_v, pooled_t, w_v, go_v, delta, own_v, row_v, lw_v, len_v, map_v, weight_v, accum_v,
     es_v, ed_v,
     fown, fsend, ybuf, gat, idx, idxb, grad, rcore, chain, rin, lin, xs, xr, place,
-    wide, inv_v, src_v, inv_s, src_s, ev_s, ev_w, ev_a, ev_g, ev_rows, ev_acc, rows_in, acc_in,
+    wide, inv_v, src_v, ev_v, inv_s, src_s, ev_s, ev_w, ev_a, ev_g, ev_rows, ev_acc, rows_in, acc_in, ev_half, half_in, ev_ok,
     ld_s, sm_s, y_s, y_r, i_s, i_r, azr_s, azl_s, ax_s, ac_s, g_r, gc_r, rc_s, rc_r,
     ch_s, ci_r, xs_s, xr_r, er_s, er_r, ea_s, ea_r, out_s, w_s,
 ):
@@ -85,18 +85,31 @@
     def cutcols(j):
         return pl.ds(j * cut, cut)
 
-    loads = [pltpu.make_async_copy(pooled, pooled_v, ld_s.at[0])]
+    def tilecols(j):
+        return pl.ds(j * tile, tile)
+
+    p_loads = [
+        pltpu.make_async_copy(pooled.at[spanb(k)], pooled_v.at[spanb(k)], ld_s.at[k])
+        for k in range(BLOCKS)
+    ]
+    base = BLOCKS
     w_loads = [
-        pltpu.make_async_copy(
-            w_up.at[:, pl.ds(j * tile, tile)], w_v.at[:, pl.ds(j * tile, tile)], ld_s.at[1 + j]
-        )
+        pltpu.make_async_copy(w_up.at[:, tilecols(j)], w_v.at[:, tilecols(j)], ld_s.at[base + j])
         for j in range(tiles)
     ]
+    base = base + tiles
+    g_first = [
+        pltpu.make_async_copy(
+            grad_out.at[spanb(0), tilecols(j)], go_v.at[spanb(0), tilecols(j)], ld_s.at[base + j]
+        )
+        for j in range(tiles)
+    ]
+    base = base + tiles
     g_loads = [
-        pltpu.make_async_copy(grad_out.at[spanb(k)], go_v.at[spanb(k)], ld_s.at[1 + tiles + k])
-        for k in range(BLOCKS)
+        pltpu.make_async_copy(grad_out.at[spanb(k)], go_v.at[spanb(k)], ld_s.at[base + k - 1])
+        for k in range(1, BLOCKS)
     ]
-    base = 1 + tiles + BLOCKS
+    base = base + BLOCKS - 1
     small = [
         pltpu.make_async_copy(src, dst, ld_s.at[base + k])
         for k, (src, dst) in enumerate((
@@ -105,9 +118,9 @@
             (accum, accum_v), (weight, weight_v),
         ))
     ]
-    loads[0].start()
+    p_loads[0].start()
     w_loads[0].start()
-    g_loads[0].start()
+    g_first[0].start()
     barrier = pltpu.get_barrier_semaphore()
 
     def greet(d, carry):
@@ -121,7 +134,10 @@
         pl.semaphore_signal(
             barrier, inc=1, device_id={"hst": lax.rem(h + d, nh)}, device_id_type=MESH
         )
-    for copy in w_loads[1:] + g_loads[1:]:
+    for j in range(1, tiles):
+        w_loads[j].start()
+        g_first[j].start()
+    for copy in p_loads[1:] + small + g_loads:
         copy.start()
 
     def y_copy(d, k):
@@ -138,10 +154,13 @@
         )
 
     def deltas(k):
-        g_loads[k].wait()
+        p_loads[k].wait()
+        if k > 0:
+            g_loads[k - 1].wait()
         for j in range(tiles):
             if k == 0:
                 w_loads[j].wait()
+                g_first[j].wait()
             cs = pl.ds(j * tile, tile)
             p = jnp.dot(pooled_v[spanb(k), :], w_v[:, cs], preferred_element_type=F32)
             s = jax.nn.sigmoid(p)
@@ -157,7 +176,11 @@
             fsend[d - 1, spanb(k)] = part.astype(BF16)
             if k == 0 and d == 1:
                 pl.semaphore_wait(barrier, n - 1 + nh - 1)
-            for q in range(SUBS):
+            y_copy(d, k * SUBS).start()
+
+    def feats_rest(k):
+        for q in range(1, SUBS):
+            for d in range(1, nh):
                 y_copy(d, k * SUBS + q).start()
 
     def feats_own(k):
@@ -165,15 +188,14 @@
             delta[spanb(k), :], w_v[cols(h), :], NT_DIMS, preferred_element_type=F32
         )
 
-    loads[0].wait()
-    deltas(0)
-    feats_out(0)
-    for copy in small:
-        copy.start()
-    feats_own(0)
-    deltas(1)
-    feats_out(1)
-    feats_own(1)
+    def i_copy(d):
+        o = lax.rem(me + d, n)
+        return rcopy(idx.at[o], idxb.at[me], i_s, i_r.at[zx], {"tbl": o})
+
+    def i_arrival(first, count):
+        ref = idxb.at[pl.ds(first, count)]
+        return rcopy(ref, ref, i_s, i_r.at[first // 2], {"tbl": at(z, x, other)})
+
 
     def g_copy(slot, k, sem, dev):
         ref = gat.at[slot, span(k)]
@@ -189,9 +211,20 @@
     def x_copy(zi, d, k):
         return g_copy(at(zi, x, c), k, ax_s, at(z, xof(d), c))
 
+    both = jnp.minimum(z, nz - 1 - z)
+
+    def ring(e):
+        dist = (e + 1) // 2
+        near = jnp.where(lax.rem(e, 2) == 1, z - dist, z + dist)
+        dist = e - both
+        far = jnp.where(z - dist >= 0, z - dist, z + dist)
+        return jnp.where(e <= 2 * both, near, far)
+
     def c_copy(zi, xi, k):
         ref = gat.at[at(zi, xi, c), span(k)]
-        return rcopy(ref, ref, ac_s, gc_r.at[zi * nx + xi], {"tbl": at(z, x, other)})
+        late = (zi == ring(nz - 1)) & (xi != x)
+        spot = jnp.where(late, nz * nx + 2 * xi + k // (PIECES // 2), zi * nx + xi)
+        return rcopy(ref, ref, ac_s, gc_r.at[spot], {"tbl": at(z, x, other)})
 
     def arrived(slot, k):
         g_copy(slot, k, ac_s, at(z, x, other)).wait_recv()
@@ -225,15 +258,8 @@
         grad[j] = part.reshape(nz, nx, 2, out_rows, cut)
         core_copy(j).start()
 
-    def i_copy(d):
-        o = lax.rem(me + d, n)
-        return rcopy(idx.at[o], idxb.at[me], i_s, i_r.at[zx], {"tbl": o})
-
-    def i_arrival(first, count):
-        ref = idxb.at[pl.ds(first, count)]
-        return rcopy(ref, ref, i_s, i_r.at[first // 2], {"tbl": at(z, x, other)})
-
-    gather_start(0)
+    deltas(0)
+    feats_out(0)
     for copy in small:
         copy.wait()
     for t in range(tables):
@@ -251,8 +277,15 @@
         return carry
 
     lax.fori_loop(1, n, i_start, 0)
+
+    feats_own(0)
+    feats_rest(0)
+    deltas(1)
+    feats_out(1)
+    feats_rest(1)
+    gather_start(0)
+    feats_own(1)
     pooled_t[...] = pooled_v[...].T
-
     weight_grad(0)
     for k in range(1, PIECES):
         gather_start(k)
@@ -261,9 +294,10 @@
     place[...] = jnp.zeros_like(place)
     chunk = min(RADIX, rows_dev)
 
-    def proc(*picked):
-        codes = [idxb[slot] for slot in picked]
-        bags = [gat[slot] for slot in picked]
+    def proc(*picked, rows_of=slice(0, batch)):
+        codes = [idxb[slot][:, rows_of] for slot in picked]
+        count = rows_of.stop - rows_of.start
+        bags = [gat[slot, pl.ds(rows_of.start, count), :] for slot in picked]
         for t in range(tables):
             pairs = []
             for code, bag_rows in zip(codes, bags):
@@ -271,7 +305,7 @@
                 row1 = jnp.floor(code * (1.0 / ROW_STEP))
                 wgt = ((code - row1 * ROW_STEP) * (1.0 / WEIGHT_STEP)).astype(BF16)
                 pairs.append((row1 - 1.0, wgt, bag_rows[:, t * emb : (t + 1) * emb]))
-            ids = iota((chunk, batch), 0).astype(F32).astype(BF16)
+            ids = iota((chunk, count), 0).astype(F32).astype(BF16)
             for r0 in range(0, rows_dev, chunk):
                 total = None
                 for row, wgt, part in pairs:
@@ -287,6 +321,7 @@
 
     inv_copy = pltpu.make_async_copy(inv_v, inv_s, sm_s.at[0])
     src_copy = pltpu.make_async_copy(src_v, src_s, sm_s.at[1])
+    ev_copy = pltpu.make_async_copy(ev_v, ev_s, sm_s.at[2])
 
     def prepare_inverse():
         home = map_v[...].astype(F32)
@@ -304,6 +339,7 @@
         inv = (found[:groups] * RADIX + found[groups:]).astype(jnp.int32)
         inv_v[...] = jnp.clip(inv, 0, slots - 1)
         inv_copy.start()
+        return found.astype(BF16)
 
 
     def prepare_wide():
@@ -311,42 +347,60 @@
             col = jnp.sum(jnp.where(eye, accum_v[i : i + 1, :], 0.0), axis=1, keepdims=True)
             wide[i * emb : (i + 1) * emb, :] = jnp.broadcast_to(col, (emb, emb))
 
-    def prepare_evict():
+    def prepare_evict(found):
         live = iota((1, list_len), 1) < evict_count[0, 0]
         lanes = 8 * -(-nh // 8)
         mine = jnp.where((iota((lanes, list_len), 0) == ed_v[...]) & live, 1.0, 0.0)
         before = jnp.where(iota((list_len, list_len), 0) < iota((list_len, list_len), 1), 1.0, 0.0)
         goal = jnp.dot(mine.astype(BF16), before.astype(BF16), preferred_element_type=F32)
-        slot1 = es_v[...].astype(F32) + 1.0
+        slot1 = es_v[...].astype(F32)
         slot_high = jnp.floor(slot1 * (1.0 / RADIX))
         slot_low = slot1 - slot_high * RADIX
         parts = jnp.where(iota((8, list_len), 0) == 0, slot_high, slot_low).astype(BF16)
         for d in range(nh):
             hot = jnp.where(
                 iota((cap, list_len), 0).astype(F32) == goal[d : d + 1], mine[d : d + 1], 0.0
-            ).astype(BF16)
+            )
+            ev_ok[d] = jnp.broadcast_to(jnp.sum(hot, axis=1, keepdims=True), (cap, emb))
+            hot = hot.astype(BF16)
             got = lax.dot_general(parts, hot, NT_DIMS, preferred_element_type=F32)
             src = (got[0:1] * RADIX + got[1:2]).astype(jnp.int32)
-            src_v[d : d + 1, :] = jnp.clip(src, 0, slots)
+            src_v[d : d + 1, :] = jnp.clip(src, 0, slots - 1)
+            from_slot = got[0:1] * RADIX + got[1:2]
+            slot_group = jnp.floor(from_slot * (1.0 / emb))
+            slot_lane = from_slot - slot_group * emb
+            lane_hot = jnp.where(iota((emb, cap), 0).astype(F32) == slot_lane, 1.0, 0.0)
+            taken = jnp.dot(found, lane_hot.astype(BF16), preferred_element_type=F32)
+            in_slot_group = iota((groups, cap), 0).astype(F32) == slot_group
+            row_high = jnp.sum(jnp.where(in_slot_group, taken[:groups], 0.0), axis=0, keepdims=True)
+            row_low = jnp.sum(jnp.where(in_slot_group, taken[groups:], 0.0), axis=0, keepdims=True)
+            ev_row = (row_high * RADIX + row_low).astype(jnp.int32)
+            ev_v[d : d + 1, :] = jnp.clip(ev_row, 0, slots - 1)
         src_copy.start()
-
-
-    def prepare_fetch(start, stop):
-        def slot_of(k, p):
-            s1 = src_s[k, p]
-            return s1 > 0, jnp.maximum(s1 - 1, 0)
-
-        def ev_fetch(i, carry):
-            k = i // (cap // 8)
-            p = lax.rem(i, cap // 8) * 8
-            for q in range(8):
-                ok, s = slot_of(k, p + q)
-                ev_w[k, pl.ds(p + q, 1), :] = jnp.where(ok, weight_v[pl.ds(s, 1), :], 0.0)
-                ev_a[k, pl.ds(p + q, 1), :] = jnp.where(ok, wide[pl.ds(s, 1), :], 0.0)
-                ev_s[k, p + q] = jnp.where(ok, inv_s[s // emb, lax.rem(s, emb)], slots)
+        ev_copy.start()
+
+
+    def gathered(ref, index):
+        return jnp.concatenate([ref[pl.ds(index(q), 1), :] for q in range(8)], axis=0)
+
+    unroll = 64
+
+    def each_evicted(body):
+        def trip(i, carry):
+            k = i // (cap // unroll)
+            p = lax.rem(i, cap // unroll) * unroll
+            for b in range(0, unroll, 8):
+                body(k, p + b, pl.ds(pl.multiple_of(p + b, 8), 8))
             return carry
 
-        lax.fori_loop(start, stop, ev_fetch, 0)
+        lax.fori_loop(0, nh * cap // unroll, trip, 0)
+
+    def prepare_fetch():
+        def fetch(k, p, rows_p):
+            ev_w[k, rows_p, :] = gathered(weight_v, lambda q: src_s[k, p + q])
+            ev_a[k, rows_p, :] = gathered(wide, lambda q: src_s[k, p + q])
+
+        each_evicted(fetch)
 
     def rin_copy(t, j):
         return rcopy(
@@ -433,15 +487,6 @@
         for dx in range(1, nx):
             x_copy(zi, dx, k).start()
         c_copy(zi, x, k).start()
-
-    both = jnp.minimum(z, nz - 1 - z)
-
-    def ring(e):
-        dist = (e + 1) // 2
-        near = jnp.where(lax.rem(e, 2) == 1, z - dist, z + dist)
-        dist = e - both
-        far = jnp.where(z - dist >= 0, z - dist, z + dist)
-        return jnp.where(e <= 2 * both, near, far)
 
     def from_x(i):
         head = i < PIECES
@@ -480,6 +525,16 @@
         rcopy(ref, ref, ac_s, gc_r.at[zi * nx + xi], {"tbl": at(z, x, other)}).wait_recv()
         return slot
 
+    halves = [slice(0, batch // 2), slice(batch // 2, batch)]
+    final = ring(nz - 1)
+
+    def core_half(xi, q):
+        slot = at(final, xi, other)
+        ref = gat.at[slot, pl.ds(q * (batch // 2), batch // 2)]
+        core = {"tbl": at(z, x, other)}
+        rcopy(ref, ref, ac_s, gc_r.at[nz * nx + 2 * xi + q], core).wait_recv()
+        return slot
+
     def pair_proc(zi, xi):
         mine = expect(zi, xi)
         proc(mine, core_slot(zi, xi))
@@ -513,38 +568,47 @@
             lin_arrival(t, k).wait_recv()
             chain_step(t, k, lin, lin_copy)
 
-        @pl.when(s == nz - 1)
+        @pl.when((s == nz - 1) & (k < CUTS - 1))
         def _():
             finish_cut(k)
 
+        @pl.when(i == 0)
+        def _():
+            found = prepare_inverse()
+            prepare_wide()
+            prepare_evict(found)
+
         @pl.when(i == 1)
         def _():
             chain_heads()
-            prepare_inverse()
-
-        @pl.when(i == 2)
-        def _():
-            prepare_wide()
-
-        @pl.when(i == 3)
-        def _():
-            prepare_evict()
 
         @pl.when(i == 2 * PIECES - 1)
         def _():
             inv_copy.wait()
             src_copy.wait()
-            prepare_fetch(0, nh * cap // 16)
-
-        @pl.when(i == 3 * PIECES - 1)
-        def _():
-            prepare_fetch(nh * cap // 16, nh * cap // 8)
+            ev_copy.wait()
+            prepare_fetch()
+
+        @pl.when(i == PIECES * nz - 2)
+        def _():
+            def one(dx, carry):
+                xi = xof(dx)
+                proc(expect(final, xi), core_half(xi, 0), rows_of=halves[0])
+                return carry
+
+            lax.fori_loop(1, nx, one, 0)
 
         side = lax.rem(k, 2) == 0
         near = k < 2
-        zi = jnp.where(near, jnp.where(side, z - s, z + s), ring(jnp.maximum(s - 1, 0)))
-        on_line = near & ((s >= 1) | side) & (zi >= 0) & (zi < nz)
-        on_side = (k == 2) & (s >= 1)
+        end = s == nz - 1
+        below = z - s
+        line = jnp.where(side & ((below >= 0) | ~end) & (s >= 1), below, z + s)
+        near = near & ((side & (s >= 1)) | (~side & ~end))
+        on_line = near & (line >= 0) & (line < nz)
+        zi = jnp.where(on_line, line, ring(jnp.maximum(s - 1, 0)))
+        half_pair = (lax.rem(s, 2) == 0) & (s - 1 <= 2 * both)
+        at_rim = jnp.where((below >= 0) | (z + s < nz), 1, 0)
+        on_side = (k == jnp.where(end, at_rim, jnp.where(half_pair, 3, 2))) & (s >= 1)
 
         @pl.when(on_line | on_side)
         def _():
@@ -552,32 +616,27 @@
                 pair_proc(zi, xof(dx))
                 return carry
 
-            lax.fori_loop(jnp.where(near, 0, 1), jnp.where(near, 1, nx), one, 0)
+            lax.fori_loop(jnp.where(on_line, 0, 1), jnp.where(on_line, 1, nx), one, 0)
 
         return carry
 
     lax.fori_loop(0, PIECES * nz, step_body, 0)
+    if nx == 1:
+        finish_cut(CUTS - 1)
     for dx in range(1, nx):
-        proc(expect(ring(nz - 1), xof(dx)))
-        proc(core_slot(ring(nz - 1), xof(dx)))
-
-    def gathered(first):
-        picks = []
-        for q in range(8):
-            picks.append(place[pl.ds(first(q), 1), :])
-        return jnp.concatenate(picks, axis=0)
-
-    def ev_gather(i, carry):
-        k = i // (cap // 8)
-        p = lax.rem(i, cap // 8) * 8
-        ev_g[k, pl.ds(pl.multiple_of(p, 8), 8), :] = gathered(lambda q: ev_s[k, p + q])
-        return carry
-
-    lax.fori_loop(0, nh * cap // 8, ev_gather, 0)
+        proc(at(final, xof(dx), c), rows_of=halves[1])
+        if dx == 1:
+            finish_cut(CUTS - 1)
+        proc(core_half(xof(dx), 1), rows_of=halves[1])
+
+    def ev_gather(k, p, rows_p):
+        ev_g[k, rows_p, :] = gathered(place, lambda q: ev_s[k, p + q])
+
+    each_evicted(ev_gather)
 
     def er_copy(d, slot):
         k = lax.rem(h + d, nh)
-        return rcopy(ev_rows.at[k], rows_in.at[slot], er_s, er_r.at[slot], {"hst": k})
+        return rcopy(ev_half.at[k], half_in.at[slot], er_s, er_r.at[slot], {"hst": k})
 
     def ea_copy(d, slot):
         k = lax.rem(h + d, nh)
@@ -589,11 +648,15 @@
             span_k = pl.ds(r0, emb)
             g = ev_g[k, span_k]
             acc = ev_a[k, span_k] + jnp.mean(g * g, axis=1, keepdims=True)
-            ev_rows[k, span_k] = ev_w[k, span_k] - LEARN_RATE * g / (jnp.sqrt(acc) + EPSILON)
-            ev_acc[k, :, span_k] = jnp.sum(jnp.where(eye, acc, 0.0), axis=0, keepdims=True)
+            left = ev_w[k, span_k] - LEARN_RATE * g / (jnp.sqrt(acc) + EPSILON)
+            used = ev_ok[k, span_k] > 0.5
+            ev_rows[k, span_k] = jnp.where(used, left, 0.0)
+            ev_acc[k, :, span_k] = jnp.sum(jnp.where(eye & used, acc, 0.0), axis=0, keepdims=True)
         if d < nh:
+            ev_half[k] = ev_rows[k].astype(BF16)
             er_copy(d, h).start()
             ea_copy(d, h).start()
+
     def held_out(buf, acc, k):
         return (
             pltpu.make_async_copy(buf.at[k], held_rows_o.at[k], out_s.at[2 + k]),
@@ -616,7 +679,7 @@
             total = jnp.zeros((8, emb), F32)
             for b in range(emb // 8):
                 rows_b = pl.ds(pl.multiple_of(i * emb + b * 8, 8), 8)
-                g = gathered(lambda q: inv_s[i, b * 8 + q])
+                g = gathered(place, lambda q: inv_s[i, b * 8 + q])
                 acc = wide[rows_b, :] + jnp.mean(g * g, axis=1, keepdims=True)
                 new_weight[rows_b, :] = weight_v[rows_b, :] - LEARN_RATE * g / (
                     jnp.sqrt(acc) + EPSILON
@@ -645,6 +708,7 @@
         k = lax.rem(h + d, nh)
         er_copy(d, k).wait_recv()
         ea_copy(d, k).wait_recv()
+        rows_in[k] = half_in[k].astype(F32)
         for copy in held_out(rows_in, acc_in, k):
             copy.start()
 
@@ -654,7 +718,7 @@
     core_dev = {"tbl": at(z, x, other)}
     if nh > 1:
         host_dev = {"hst": lax.rem(h + 1, nh)}
-        all_sent(ev_rows.at[pl.ds(0, nh - 1)], er_s, er_r.at[0], host_dev)
+        all_sent(ev_half.at[pl.ds(0, nh - 1)], er_s, er_r.at[0], host_dev)
         all_sent(ev_acc.at[pl.ds(0, nh - 1)], ea_s, ea_r.at[0], host_dev)
         all_sent(fsend, y_s, y_r.at[0, 0], host_dev)
     all_sent(rcore, rc_s, rc_r, core_dev)
@@ -759,9 +823,10 @@
             pltpu.VMEM((nz, CUTS, nx, out_rows, cut), BF16),
             pltpu.VMEM((max(nx - 1, 1), CUTS, out_rows, cut), BF16),
             pltpu.VMEM((nx, CUTS, out_rows, cut), BF16),
-            pltpu.VMEM((slots + 8, emb), F32),
+            pltpu.VMEM((slots, emb), F32),
             pltpu.VMEM((slots, emb), F32),
             pltpu.VMEM((groups, emb), i32),
+            pltpu.VMEM((nh, cap), i32),
             pltpu.VMEM((nh, cap), i32),
             pltpu.SMEM((groups, emb), i32),
             pltpu.SMEM((nh, cap), i32),
@@ -773,9 +838,12 @@
             pltpu.VMEM((nh, 1, cap), F32),
             pltpu.VMEM((nh, cap, emb), F32),
             pltpu.VMEM((nh, 1, cap), F32),
-            dma((1 + hid // tile + BLOCKS + 9,)), dma((2,)),
+            pltpu.VMEM((nh, cap, emb), BF16),
+            pltpu.VMEM((nh, cap, emb), BF16),
+            pltpu.VMEM((nh, cap, emb), F32),
+            dma((2 * (hid // tile) + 2 * BLOCKS - 1 + 11,)), dma((3,)),
             dma, dma((max(nh - 1, 1), PIECES)), dma, dma((nz * nx,)),
-            dma, dma, dma, dma, dma((nz * nx, PIECES)), dma((nz * nx,)), dma, dma,
+            dma, dma, dma, dma, dma((nz * nx, PIECES)), dma((nz * nx + 2 * nx,)), dma, dma,
             dma, dma((nz + 1, CUTS)), dma, dma((max(nx - 1, 1),)),
             dma, dma((nh,)), dma, dma((nh,)), dma((2 + 2 * nh,)), dma,
         ],

time: 45.5 us -> 43 us (0.945)
  Pallas kernels: 44.1 us -> 41.4 us
    pallas_call x1, Pallas kernels: 42.9 us -> 40.2 us  [on_device(): pl.pallas_call(functools.partial(step_kernel, nz, nx, nh, tables, rows_de...]
where the time goes in v4:
time: 43 us; the launch traced here: 42.7 us
  Pallas kernels  41.4 us (96%)
  between operations  1.29 us (3%)
    pallas_call x1, Pallas kernels, on_device(): pl.pallas_call(functools.partial(step_kernel, nz, nx, nh, tables, rows_de...  40.2 us
    pallas_call x1, Pallas kernels, on_device(): pl.pallas_call(write_kernel, out_shape=tuple((jax.ShapeDtypeStruct(v.shap...  1.14 us

profile of v4, /device:TPU:0, one launch (start us, length us, event | category | flops | bytes accessed | tf_op | source)
XLA Modules:
  0.0 42.7 jit_solution(7736599176617569524)
XLA Ops:
  1.3 40.2 %step.1 = (f32[32,2048]{1,0:T(8,128)S(1)}, f32[2048,128]{1,0:T(8,128)S(1)}, f32[16,128]{1,0:T(8,128)S(1)}, f32[2,128,128]{2,1,0:T(8,128)S(1)}, f32[2,1,128]{2,1,0:T(1,128)S(1)}) custom-call(bf16[512,512]{1,0:T(8,128)(2,1)} %pooled.1, bf16[512,2048]{1,0:T(8,128)(2,1)} %w_up.1, bf16[512,2048]{1,0:T(8,128)(2,1)} %grad_out.1, s32[2,8,512]{2,1,0:T(8,128)} %bitcast.13, ...), custom_call_target="tpu_custom_call" | custom-call | tf_op jit(solution)/shard_map/step/pallas_call | solution.py:784
  41.5 1.1 %write.1 = (f32[32,2048]{1,0:T(8,128)}, f32[2048,128]{1,0:T(8,128)}, f32[16,128]{1,0:T(8,128)}, f32[2,128,128]{2,1,0:T(8,128)}, f32[2,1,128]{2,1,0:T(1,128)}) custom-call(f32[32,2048]{1,0:T(8,128)S(1)} %get-tuple-element.15.refs_0_, f32[2048,128]{1,0:T(8,128)S(1)} %get-tuple-element.16.refs_1_, f32[16,128]{1,0:T(8,128)S(1)} %get-tuple-element.17.refs_2_, ...), custom_call_target="tpu_custom_call" | custom-call | tf_op jit(solution)/shard_map/write/pallas_call | solution.py:863

commit v5 on v4

--- a/solution.py
+++ b/solution.py
@@ -14,7 +14,7 @@
 SUBS = 2
 PIECES = BLOCKS * SUBS
 CUTS = 4
-UPDATE_TILES = 4
+UPDATE_TILES = 8
 RADIX = 256
 ROW_STEP = 2048.0
 WEIGHT_STEP = 512.0
@@ -624,10 +624,9 @@
     if nx == 1:
         finish_cut(CUTS - 1)
     for dx in range(1, nx):
-        proc(at(final, xof(dx), c), rows_of=halves[1])
         if dx == 1:
             finish_cut(CUTS - 1)
-        proc(core_half(xof(dx), 1), rows_of=halves[1])
+        proc(at(final, xof(dx), c), core_half(xof(dx), 1), rows_of=halves[1])
 
     def ev_gather(k, p, rows_p):
         ev_g[k, rows_p, :] = gathered(place, lambda q: ev_s[k, p + q])
@@ -666,7 +665,7 @@
     for copy in held_out(ev_rows, ev_acc, h):
         copy.start()
 
-    batch_tiles = max(u for u in (1, 2, UPDATE_TILES) if groups % u == 0)
+    batch_tiles = max(u for u in (1, 2, 4, UPDATE_TILES) if groups % u == 0)
     spread = batch_tiles * emb
 
     def weight_out(i):

time: 43 us -> 43 us (level)
  no operation moved by 1% of the time
where the time goes in v5:
time: 43 us; the launch traced here: 42.6 us
  Pallas kernels  41.3 us (96%)
  between operations  1.29 us (3%)
    pallas_call x1, Pallas kernels, on_device(): pl.pallas_call(functools.partial(step_kernel, nz, nx, nh, tables, rows_de...  40.1 us
    pallas_call x1, Pallas kernels, on_device(): pl.pallas_call(write_kernel, out_shape=tuple((jax.ShapeDtypeStruct(v.shap...  1.14 us

profile of v5, /device:TPU:0, one launch (start us, length us, event | category | flops | bytes accessed | tf_op | source)
XLA Modules:
  0.0 42.6 jit_solution(12443546261319641197)
XLA Ops:
  1.3 40.1 %step.1 = (f32[32,2048]{1,0:T(8,128)S(1)}, f32[2048,128]{1,0:T(8,128)S(1)}, f32[16,128]{1,0:T(8,128)S(1)}, f32[2,128,128]{2,1,0:T(8,128)S(1)}, f32[2,1,128]{2,1,0:T(1,128)S(1)}) custom-call(bf16[512,512]{1,0:T(8,128)(2,1)} %pooled.1, bf16[512,2048]{1,0:T(8,128)(2,1)} %w_up.1, bf16[512,2048]{1,0:T(8,128)(2,1)} %grad_out.1, s32[2,8,512]{2,1,0:T(8,128)} %bitcast.13, ...), custom_call_target="tpu_custom_call" | custom-call | tf_op jit(solution)/shard_map/step/pallas_call | solution.py:783
  41.4 1.1 %write.1 = (f32[32,2048]{1,0:T(8,128)}, f32[2048,128]{1,0:T(8,128)}, f32[16,128]{1,0:T(8,128)}, f32[2,128,128]{2,1,0:T(8,128)}, f32[2,1,128]{2,1,0:T(1,128)}) custom-call(f32[32,2048]{1,0:T(8,128)S(1)} %get-tuple-element.15.refs_0_, f32[2048,128]{1,0:T(8,128)S(1)} %get-tuple-element.16.refs_1_, f32[16,128]{1,0:T(8,128)S(1)} %get-tuple-element.17.refs_2_, ...), custom_call_target="tpu_custom_call" | custom-call | tf_op jit(solution)/shard_map/write/pallas_call | solution.py:862
